TPU v7x, 256 devices: a whole 4x4x8 slice. The times are simulated.
256 devices in a mesh: pipe: 4 (over z_lo), expert: 64 (over y, z_hi, x, core).
Axes of the slice: x: 4, y: 4, z: 8 (z_hi: 2, z_lo: 4; z = z_hi * 4 + z_lo), core: 2. Of those that a mesh axis runs over, the one named last changes fastest.
Arguments:
- tokens: bfloat16 [32768, 3584], P(('pipe', 'expert')), may hold values from -6 to 6
- out_grad: bfloat16 [32768, 3584], P(('pipe', 'expert')), may hold values from -6 to 6
- probs: bfloat16 [32768, 8], P(('pipe', 'expert')), may hold values from 0.049804688 to 1
- expert_ids: int32 [32768, 8], P(('pipe', 'expert')), may hold values from 0 to 255, as said below
- w_gate: bfloat16 [4, 3584, 16384], P('pipe', None, 'expert'), as said below
- w_up: bfloat16 [4, 3584, 16384], P('pipe', None, 'expert'), as said below
- w_down: bfloat16 [4, 16384, 3584], P('pipe', 'expert'), as said below
Outputs:
- tokens_grad: bfloat16 [32768, 3584], P(('pipe', 'expert'))
- weight_grads: bfloat16 [4, 3, 1792, 16384], P('pipe', None, None, 'expert')
Inputs may be any that keep to these rules, and one draw needn't show every extreme that they name: `expert_ids`: each row names 8 different experts. Experts 8 and above lie outside this window. Among the 128 tokens of one device (aligned blocks of rows), each expert below 8 is named by at most 8 tokens, and in every draw one such expert is named by exactly 8 tokens on every device. `w_gate`: entries k and 3 - k along the first dimension are equal. `w_up`: entries k and 3 - k along the first dimension are equal. `w_down`: entries k and 3 - k along the first dimension are equal.
All inputs are finite; a program needn't handle non-finite values.
Results may differ from a plain program's by a relative error of at most 0.0065.
Values may be sent and summed in bfloat16 or wider, within the bound.
No kernel may reach another device: no remote copies, remote signals or barrier semaphores. Data moves between devices by JAX's collectives and lax.ppermute only.
A program may use at most 128 MiB of HBM per device.

v0:
```python
import jax
import jax.numpy as jnp
from jax import lax
from jax.sharding import PartitionSpec as P

GROUP = 8
CAP = 8


def from_partner(value, axis, apart):
    mask = 2**apart
    pairs = [(source, source ^ mask) for source in range(lax.axis_size(axis))]
    return lax.ppermute(value, axis, pairs)


def route_slots(block_ids, block_probs, in_flight):
    experts = jnp.arange(in_flight, dtype=jnp.int32)
    hits = block_ids[:, :, None] == experts[None, None, :]
    member = jnp.any(hits, axis=1).astype(jnp.int32)
    chosen = jnp.sum(
        jnp.where(hits, block_probs.astype(jnp.float32)[:, :, None], jnp.float32(0.0)), axis=1
    )
    position = jnp.cumsum(member, axis=0) - member
    slots = jnp.arange(CAP, dtype=jnp.int32)
    select = (member.T[:, None, :] == 1) & (position.T[:, None, :] == slots[None, :, None])
    select = select.astype(jnp.float32)
    slot_weight = jnp.einsum("ect,te->ec", select, chosen, precision=lax.Precision.HIGHEST)
    return (select.reshape(in_flight * CAP, -1), slot_weight.reshape(in_flight * CAP))


def contract(left, right, left_dim, right_dim):
    return lax.dot_general(
        left, right, (((left_dim,), (right_dim,)), ((), ())), preferred_element_type=jnp.float32
    )


def expert_backward(x_rows, grad_rows, gate_cols, up_cols, down_rows):
    gate = jnp.dot(x_rows, gate_cols, preferred_element_type=jnp.float32)
    up = jnp.dot(x_rows, up_cols, preferred_element_type=jnp.float32)
    sigmoid_gate = jax.nn.sigmoid(gate)
    activated = gate * sigmoid_gate
    hidden = (activated * up).astype(jnp.bfloat16)
    back = contract(grad_rows, down_rows, 1, 1)
    d_gate = (back * up * sigmoid_gate * (1.0 + gate * (1.0 - sigmoid_gate))).astype(jnp.bfloat16)
    d_up = (back * activated).astype(jnp.bfloat16)
    row_grad = contract(d_gate, gate_cols, 1, 1) + contract(d_up, up_cols, 1, 1)
    grads = jnp.stack(
        [
            contract(x_rows, d_gate, 0, 0),
            contract(x_rows, d_up, 0, 0),
            contract(grad_rows, hidden, 0, 0),
        ]
    ).astype(jnp.bfloat16)
    return (row_grad, grads)


def body(tokens, out_grad, probs, expert_ids, w_gate, w_up, w_down):
    axis_width = lax.axis_size("expert")
    in_flight = axis_width // GROUP
    features = tokens.shape[1]
    select, slot_weight = route_slots(expert_ids, probs, in_flight)
    picker = select.astype(jnp.bfloat16)
    x_rows = jnp.dot(picker, tokens, preferred_element_type=jnp.float32).astype(jnp.bfloat16)
    grad_rows = (
        jnp.dot(picker, out_grad, preferred_element_type=jnp.float32) * slot_weight[:, None]
    ).astype(jnp.bfloat16)
    stacked = jnp.stack([x_rows, grad_rows])
    outgoing = jnp.broadcast_to(
        stacked.reshape(2, in_flight, 1, CAP, features), (2, in_flight, GROUP, CAP, features)
    )
    outgoing = outgoing.reshape(2, axis_width, CAP, features)
    arrived = lax.all_to_all(outgoing, "expert", split_axis=1, concat_axis=1, tiled=True)
    arrived = arrived.reshape(2, axis_width * CAP, features)
    row_grad, grads = expert_backward(arrived[0], arrived[1], w_gate[0], w_up[0], w_down[0])
    returned = lax.all_to_all(
        row_grad.reshape(axis_width, CAP, features),
        "expert",
        split_axis=0,
        concat_axis=0,
        tiled=True,
    )
    summed = jnp.sum(returned.reshape(in_flight, GROUP, CAP, features), axis=1).reshape(
        in_flight * CAP, features
    )
    tokens_grad = lax.dot_general(
        select,
        summed,
        (((0,), (0,)), ((), ())),
        precision=lax.Precision.HIGHEST,
        preferred_element_type=jnp.float32,
    )
    tokens_grad = tokens_grad.astype(jnp.bfloat16)
    half_rows = features // 2
    section_count = lax.axis_size("pipe")
    section_bits = section_count.bit_length() - 1
    lower_section = lax.axis_index("pipe") < section_count // 2
    retained_grads = jnp.where(lower_section, grads[:, :half_rows], grads[:, half_rows:])
    incoming = jnp.where(lower_section, grads[:, half_rows:], grads[:, :half_rows])
    for level in range(section_bits):
        incoming = from_partner(incoming, "pipe", level)
    weight_grads = (retained_grads.astype(jnp.float32) + incoming.astype(jnp.float32)).astype(
        jnp.bfloat16
    )
    return (tokens_grad, weight_grads[None])


def solution(mesh):
    return jax.shard_map(
        body,
        mesh=mesh,
        in_specs=(
            P(("pipe", "expert"), None),
            P(("pipe", "expert"), None),
            P(("pipe", "expert"), None),
            P(("pipe", "expert"), None),
            P("pipe", None, "expert"),
            P("pipe", None, "expert"),
            P("pipe", "expert", None),
        ),
        out_specs=(P(("pipe", "expert"), None), P("pipe", None, None, "expert")),
        check_vma=False,
    )
```

profile of v0, /device:TPU:33, one launch (start us, length us, event | category | flops | bytes accessed | tf_op | source)
XLA Modules:
  0.0 550.9 jit_solution(7055015757584703618)
XLA Ops:
  0.6 0.8 fusion.19
  1.5 0.7 convert_element_type.48
  2.2 0.7 select_reduce_fusion
  2.9 0.1 eq.58
  2.9 0.1 copy.18
  3.2 0.2 reduce_window_sum.11
  3.4 0.2 fusion.22
  3.7 1.5 fusion.6
  5.2 1.5 fusion.5
  6.7 0.1 maximum_bitcast_fusion
  6.9 0.9 broadcast_in_dim.31
  7.8 181.0 %all_to_all.10 = bf16[2,64,8,3584]{3,2,0,1:T(8,128)(2,1)S(1)} all-to-all(bf16[2,64,8,3584]{3,2,0,1:T(8,128)(2,1)S(1)} %bitcast.79), channel_id=1, replica_groups=mesh['pipe'=4,'expert'=64] {'expert'}, dimensions={1} | all-to-all | bytes 14680064 | tf_op jit(solution)/shard_map/all_to_all | solution.py:72
  188.8 1.1 fusion.9
  189.9 1.7 copy-done.3
  191.6 1.1 fusion.10
  192.8 0.6 copy-done.4
  193.4 1.2 multiply_convert_fusion.1
  194.6 1.1 fusion.11
  195.8 4.2 add_bitcast_fusion
  200.0 5.6 %all-to-all-start.1 = ((f32[64,8,3584]{2,1,0:T(8,128)}), f32[64,8,3584]{2,1,0:T(8,128)}, u32[]{:S(2)}, u32[]{:S(2)}) async-start(f32[64,8,3584]{2,1,0:T(8,128)} %add_bitcast_fusion), calls=%async_computation.1 | async-start | bytes 14680064 | tf_op jit(solution)/shard_map/all_to_all | solution.py:75
  205.7 3.4 fusion.1
  209.0 3.4 fusion
  212.4 1.3 fusion.2
  213.8 0.7 pad_maximum_fusion
  214.4 0.3 broadcast_select_fusion
  214.7 0.1 collective-permute-start
  214.8 206.9 %collective-permute-done = bf16[3,1792,256]{2,1,0:T(8,128)(2,1)S(1)} collective-permute-done((bf16[3,1792,256]{2,1,0:T(8,128)(2,1)S(1)}, bf16[3,1792,256]{2,1,0:T(8,128)(2,1)S(1)}, u32[]{:S(2)}, u32[]{:S(2)}) %collective-permute-start) | collective-permute-done | bytes 2752544 | tf_op jit(solution)/shard_map/ppermute | solution.py:13
  421.7 3.6 collective-permute-start.1
  425.3 117.6 %collective-permute-done.1 = bf16[3,1792,256]{2,1,0:T(8,128)(2,1)S(1)} collective-permute-done((bf16[3,1792,256]{2,1,0:T(8,128)(2,1)S(1)}, bf16[3,1792,256]{2,1,0:T(8,128)(2,1)S(1)}, u32[]{:S(2)}, u32[]{:S(2)}) %collective-permute-start.1) | collective-permute-done | bytes 2752544 | tf_op jit(solution)/shard_map/ppermute | solution.py:13
  542.8 2.6 fusion.8
  545.4 3.7 bitcast_reduce_fusion
  549.1 1.9 fusion.3
  (21 shorter events, 0.3 us)
Async XLA Ops:
  0.6 188.1 %copy-start = (bf16[1,3584,256]{2,1,0:T(8,128)(2,1)S(1)}, bf16[1,3584,256]{2,1,0:T(8,128)(2,1)}, u32[]{:S(2)}) copy-start(bf16[1,3584,256]{2,1,0:T(8,128)(2,1)} %param.11) | copy-start | bytes 5505028
  188.8 4.0 copy-start.2
  188.8 2.9 copy-start.3
  191.6 1.8 copy-start.4
  200.0 345.4 %all-to-all-start.1 = ((f32[64,8,3584]{2,1,0:T(8,128)}), f32[64,8,3584]{2,1,0:T(8,128)}, u32[]{:S(2)}, u32[]{:S(2)}) async-start(f32[64,8,3584]{2,1,0:T(8,128)} %add_bitcast_fusion), calls=%async_computation.1 | async-start | bytes 14680064 | tf_op jit(solution)/shard_map/all_to_all | solution.py:75
  205.6 6.7 %slice-start = ((s8[7340032]{0:T(1024)(128)(4,1)}), s8[4194304]{0:T(1024)(128)(4,1)S(1)}, s32[]{:S(2)}) async-start(s8[7340032]{0:T(1024)(128)(4,1)} %bitcast.80), calls=%async_computation.2 | async-start | bytes 8388608
  209.0 3.4 slice-start.1
  214.7 207.0 %collective-permute-start = (bf16[3,1792,256]{2,1,0:T(8,128)(2,1)S(1)}, bf16[3,1792,256]{2,1,0:T(8,128)(2,1)S(1)}, u32[]{:S(2)}, u32[]{:S(2)}) collective-permute-start(bf16[3,1792,256]{2,1,0:T(8,128)(2,1)S(1)} %broadcast_select_fusion), channel_id=1, source_target_pairs={{0,64},{64,0},{128,192},{192,128},{1,65},{65,1},{129,193},{193,129... | collective-permute-start | bytes 8257544 | tf_op jit(solution)/shard_map/ppermute | solution.py:13
  421.7 121.1 %collective-permute-start.1 = (bf16[3,1792,256]{2,1,0:T(8,128)(2,1)S(1)}, bf16[3,1792,256]{2,1,0:T(8,128)(2,1)S(1)}, u32[]{:S(2)}, u32[]{:S(2)}) collective-permute-start(bf16[3,1792,256]{2,1,0:T(8,128)(2,1)S(1)} %collective-permute-done), channel_id=1, source_target_pairs={{0,128},{64,192},{128,0},{192,64},{1,129},{65,193},{129,1},{193,65... | collective-permute-start | bytes 8257544 | tf_op jit(solution)/shard_map/ppermute | solution.py:13
  542.8 8.1 %copy-start.1 = (bf16[1,3584,256]{2,1,0:T(8,128)(2,1)S(1)}, bf16[1,3584,256]{2,1,0:T(8,128)(2,1)}, u32[]{:S(2)}) copy-start(bf16[1,3584,256]{2,1,0:T(8,128)(2,1)} %param.11) | copy-start | bytes 5505028
where the time goes:
time: 555 us; the launch traced here: 551 us
  waiting for transfers between devices  324 us (58%)
  blocking collectives  181 us (33%)
  matrix products  22 us (4%)
  other arithmetic  9.7 us (2%)
  starting transfers between devices  9.28 us (2%)
    ppermute x2, waiting for transfers between devices, from_partner(): return lax.ppermute(value, axis, pairs)  324 us
    all_to_all x1, blocking collectives, body(): lax.all_to_all(outgoing, 'expert', split_axis=1, concat_axis=1, tiled=True)  181 us
    dot_general x6, matrix products, contract(): lax.dot_general(left, right, (((left_dim,), (right_dim,)), ((), ())), pre...  14.7 us
  transfers between devices with their start and end apart: 3, of which 2 were waited for; matrix products, arithmetic and copies ran while one was open for 2% of the time, Pallas kernels for 0%

commit v1 on v0

v1 whole, which is shorter than its diff:
```python
import jax
import jax.numpy as jnp
from jax import lax
from jax.sharding import PartitionSpec as P

GROUP = 8
CAP = 8
CORES = 2
CHIPS = GROUP // CORES


def route_slots(block_ids, block_probs, in_flight):
    experts = jnp.arange(in_flight, dtype=jnp.int32)
    hits = block_ids[:, :, None] == experts[None, None, :]
    member = jnp.any(hits, axis=1).astype(jnp.int32)
    chosen = jnp.sum(
        jnp.where(hits, block_probs.astype(jnp.float32)[:, :, None], jnp.float32(0.0)), axis=1
    )
    position = jnp.cumsum(member, axis=0) - member
    slots = jnp.arange(CAP, dtype=jnp.int32)
    select = (member.T[:, None, :] == 1) & (position.T[:, None, :] == slots[None, :, None])
    select = select.astype(jnp.float32)
    slot_weight = jnp.einsum("ect,te->ec", select, chosen, precision=lax.Precision.HIGHEST)
    return (select.reshape(in_flight * CAP, -1), slot_weight.reshape(in_flight * CAP))


def contract(left, right, left_dim, right_dim):
    return lax.dot_general(
        left, right, (((left_dim,), (right_dim,)), ((), ())), preferred_element_type=jnp.float32
    )


def along_x(value, shift):
    width = lax.axis_size("expert")
    pairs = []
    for source in range(width):
        group, member = divmod(source, GROUP)
        chip, core = divmod(member, CORES)
        pairs.append((source, group * GROUP + (chip + shift) % CHIPS * CORES + core))
    return lax.ppermute(value, "expert", pairs)


def other_core(value):
    width = lax.axis_size("expert")
    return lax.ppermute(value, "expert", [(source, source ^ 1) for source in range(width)])


def mirror(value):
    count = lax.axis_size("pipe")
    return lax.ppermute(value, "pipe", [(k, count - 1 - k) for k in range(count)])


def across_groups(value):
    width = lax.axis_size("expert")
    groups = [[e * GROUP + g for e in range(width // GROUP)] for g in range(GROUP)]
    return lax.all_to_all(
        value, "expert", split_axis=0, concat_axis=0, axis_index_groups=groups, tiled=True
    )


def gather_chips(rows):
    half = rows.shape[0] // 2
    below = along_x(rows, 1)
    above = along_x(rows, -1)
    far_low = along_x(below[:half], 1)
    far_high = along_x(above[half:], -1)
    return jnp.concatenate([rows, below, above, far_low, far_high])


def body(tokens, out_grad, probs, expert_ids, w_gate, w_up, w_down):
    axis_width = lax.axis_size("expert")
    in_flight = axis_width // GROUP
    features = tokens.shape[1]
    half_rows = features // 2
    lower = lax.axis_index("pipe") < lax.axis_size("pipe") // 2
    w_gate, w_up, w_down = w_gate[0], w_up[0], w_down[0]
    bf16 = jnp.bfloat16

    select, slot_weight = route_slots(expert_ids, probs, in_flight)
    picker = select.astype(bf16)
    x_rows = jnp.dot(picker, tokens, preferred_element_type=jnp.float32).astype(bf16)
    grad_rows = (
        jnp.dot(picker, out_grad, preferred_element_type=jnp.float32) * slot_weight[:, None]
    ).astype(bf16)

    x_here = across_groups(x_rows)
    g_here = across_groups(grad_rows)

    def keep(value):
        return jnp.where(lower, value[:, :half_rows], value[:, half_rows:])

    def give(value):
        return jnp.where(lower, value[:, half_rows:], value[:, :half_rows])

    x_mine = gather_chips(x_here)
    x_other = other_core(x_mine)
    g_mine = gather_chips(g_here)
    g_other = other_core(g_mine)
    m_here = mirror(jnp.concatenate([give(x_here), give(g_here)], axis=1))
    m_mine = gather_chips(m_here)
    m_other = other_core(m_mine)

    def hidden_units(x, g):
        gate = jnp.dot(x, w_gate, preferred_element_type=jnp.float32)
        up = jnp.dot(x, w_up, preferred_element_type=jnp.float32)
        back = contract(g, w_down, 1, 1)
        s = jax.nn.sigmoid(gate)
        activated = gate * s
        hidden = (activated * up).astype(bf16)
        d_gate = (back * up * s * (1.0 + gate * (1.0 - s))).astype(bf16)
        d_up = (back * activated).astype(bf16)
        return d_gate, d_up, hidden

    x_all = jnp.concatenate([x_mine, x_other])
    g_all = jnp.concatenate([g_mine, g_other])
    d_gate, d_up, hidden = hidden_units(x_all, g_all)
    acts = jnp.stack([d_gate, d_up, hidden])
    m_acts = mirror(acts)

    row_grad = contract(d_gate, w_gate, 1, 1) + contract(d_up, w_up, 1, 1)
    n_mine = x_mine.shape[0]
    rows_dev = n_mine // CHIPS
    summed = row_grad[:n_mine] + other_core(row_grad[n_mine:].astype(bf16)).astype(jnp.float32)
    to_below = summed[rows_dev : 2 * rows_dev].astype(bf16)
    to_above = summed[2 * rows_dev : 3 * rows_dev].astype(bf16)
    to_far = summed[3 * rows_dev :].astype(bf16)
    total = (
        summed[:rows_dev]
        + along_x(to_below, -1).astype(jnp.float32)
        + along_x(to_above, 1).astype(jnp.float32)
        + along_x(to_far, 2).astype(jnp.float32)
    )
    returned = across_groups(total.astype(bf16))
    tokens_grad = contract(picker, returned, 0, 0).astype(bf16)

    x_keep = jnp.concatenate([keep(x_all), m_mine[:, :half_rows], m_other[:, :half_rows]])
    g_keep = jnp.concatenate([keep(g_all), m_mine[:, half_rows:], m_other[:, half_rows:]])
    both = jnp.concatenate([acts, m_acts], axis=1)
    weight_grads = jnp.stack(
        [
            contract(x_keep, both[0], 0, 0).astype(bf16),
            contract(x_keep, both[1], 0, 0).astype(bf16),
            contract(g_keep, both[2], 0, 0).astype(bf16),
        ]
    )
    return (tokens_grad, weight_grads[None])


def solution(mesh):
    return jax.shard_map(
        body,
        mesh=mesh,
        in_specs=(
            P(("pipe", "expert"), None),
            P(("pipe", "expert"), None),
            P(("pipe", "expert"), None),
            P(("pipe", "expert"), None),
            P("pipe", None, "expert"),
            P("pipe", None, "expert"),
            P("pipe", "expert", None),
        ),
        out_specs=(P(("pipe", "expert"), None), P("pipe", None, None, "expert")),
        check_vma=False,
    )
```

time: 555 us -> 186 us (0.34)
  waiting for transfers between devices: 324 us -> 97.3 us
  blocking collectives: 181 us -> 0 us
  starting transfers between devices: 9.28 us -> 50.1 us
    ppermute x2 -> x21, waiting for transfers between devices: 324 us -> 62.9 us  [the longest x15 34.8 us: along_x(): return lax.ppermute(value, 'expert', pairs)]
    all_to_all x1 -> x0, blocking collectives: 181 us -> none  [body(): lax.all_to_all(outgoing, 'expert', split_axis=1, concat_axis=1, tiled=True)]
    all_to_all x1 -> x3, waiting for transfers between devices: 0.01 us -> 34.5 us  [across_groups(): lax.all_to_all(value, 'expert', split_axis=0, concat_axis=0, axis_index_g...]
    ppermute x2 -> x21, starting transfers between devices: 3.67 us -> 29 us  [the longest x15 21.3 us: along_x(): return lax.ppermute(value, 'expert', pairs)]
    all_to_all x1 -> x3, starting transfers between devices: 5.61 us -> 21.1 us  [across_groups(): lax.all_to_all(value, 'expert', split_axis=0, concat_axis=0, axis_index_g...]
    dot_general x6 -> x7, matrix products: 14.7 us -> 11.8 us  [contract(): lax.dot_general(left, right, (((left_dim,), (right_dim,)), ((), ())), pre...]
  transfers between devices with their start and end apart: 3 -> 24, of which waited for: 2 -> 11; matrix products, arithmetic and copies ran while one was open for 2% -> 12% of each run, Pallas kernels for 0% -> 0%
where the time goes in v1:
time: 186 us; the launch traced here: 182 us
  waiting for transfers between devices  97.3 us (52%)
  starting transfers between devices  50.1 us (27%)
  matrix products  18.9 us (10%)
  local copies, waits for them, and re-layouts  8.51 us (5%)
  other arithmetic  6.52 us (4%)
    ppermute x15, waiting for transfers between devices, along_x(): return lax.ppermute(value, 'expert', pairs)  34.8 us
    all_to_all x3, waiting for transfers between devices, across_groups(): lax.all_to_all(value, 'expert', split_axis=0, concat_axis=0, axis_index_g...  34.5 us
    ppermute x2, waiting for transfers between devices, mirror(): lax.ppermute(value, 'pipe', [(k, count - 1 - k) for k in range(count)])  28.1 us
    ppermute x15, starting transfers between devices, along_x(): return lax.ppermute(value, 'expert', pairs)  21.3 us
    all_to_all x3, starting transfers between devices, across_groups(): lax.all_to_all(value, 'expert', split_axis=0, concat_axis=0, axis_index_g...  21.1 us
    dot_general x7, matrix products, contract(): lax.dot_general(left, right, (((left_dim,), (right_dim,)), ((), ())), pre...  11.8 us
    ppermute x4, starting transfers between devices, other_core(): lax.ppermute(value, 'expert', [(source, source ^ 1) for source in range(w...  6.27 us
    unnamed x28, local copies, waits for them, and re-layouts  4.34 us
  transfers between devices with their start and end apart: 24, of which 11 were waited for; matrix products, arithmetic and copies ran while one was open for 12% of the time, Pallas kernels for 0%

profile of v1, /device:TPU:33, one launch (start us, length us, event | category | flops | bytes accessed | tf_op | source)
XLA Modules:
  0.0 182.4 jit_solution(11498022783942746759)
XLA Ops:
  3.7 2.3 %fusion.2 = bf16[8,8,3584]{2,1,0:T(8,128)(2,1)} fusion(bf16[128,3584]{1,0:T(8,128)(2,1)} %param.8, f32[64]{0:T(128)S(1)} %mul.31, s32[64]{0:T(128)S(1)} %eq.59, s32[8,128]{1,0:T(8,128)S(1)} %copy.15, pred[8,128]{1,0:T(8,128)(4,1)S(1)} %copy.14), kind=kOutput, calls=%fused_computation.6 | convolution fusion | flops 59211776 | bytes 1381888 | tf_op jit(solution)/shard_map/dot_general | solution.py:83
  6.0 9.9 %all-to-all-start = ((bf16[8,8,3584]{2,1,0:T(8,128)(2,1)}), bf16[8,8,3584]{2,1,0:T(8,128)(2,1)S(1)}, u32[]{:S(2)}, u32[]{:S(2)}) async-start(bf16[8,8,3584]{2,1,0:T(8,128)(2,1)} %fusion.2), calls=%async_computation | async-start | bytes 917504 | tf_op jit(solution)/shard_map/all_to_all | solution.py:56
  15.9 2.3 %fusion.3 = bf16[8,8,3584]{2,1,0:T(8,128)(2,1)} fusion(bf16[128,3584]{1,0:T(8,128)(2,1)} %param.7, s32[64]{0:T(128)S(1)} %eq.59, s32[8,128]{1,0:T(8,128)S(1)} %copy.15, pred[8,128]{1,0:T(8,128)(4,1)S(1)} %copy.14), kind=kOutput, calls=%fused_computation.7 | convolution fusion | flops 58982400 | bytes 1381632 | tf_op jit(solution)/shard_map/dot_general | solution.py:81
  18.2 15.4 %all-to-all-done = bf16[8,8,3584]{2,1,0:T(8,128)(2,1)S(1)} async-done(((bf16[8,8,3584]{2,1,0:T(8,128)(2,1)}), bf16[8,8,3584]{2,1,0:T(8,128)(2,1)S(1)}, u32[]{:S(2)}, u32[]{:S(2)}) %all-to-all-start) | async-done | bytes 458784 | tf_op jit(solution)/shard_map/all_to_all | solution.py:56
  33.5 3.5 %all-to-all-start.1 = ((bf16[8,8,3584]{2,1,0:T(8,128)(2,1)}), bf16[8,8,3584]{2,1,0:T(8,128)(2,1)S(1)}, u32[]{:S(2)}, u32[]{:S(2)}) async-start(bf16[8,8,3584]{2,1,0:T(8,128)(2,1)} %fusion.3), calls=%async_computation.1 | async-start | bytes 917504 | tf_op jit(solution)/shard_map/all_to_all | solution.py:56
  38.3 1.5 collective-permute-start.1
  39.8 12.5 %all-to-all-done.1 = bf16[8,8,3584]{2,1,0:T(8,128)(2,1)S(1)} async-done(((bf16[8,8,3584]{2,1,0:T(8,128)(2,1)}), bf16[8,8,3584]{2,1,0:T(8,128)(2,1)S(1)}, u32[]{:S(2)}, u32[]{:S(2)}) %all-to-all-start.1) | async-done | bytes 458784 | tf_op jit(solution)/shard_map/all_to_all | solution.py:56
  53.5 1.5 collective-permute-start.6
  57.0 2.7 %collective-permute-start.3 = (bf16[32,3584]{1,0:T(8,128)(2,1)S(1)}, bf16[32,3584]{1,0:T(8,128)(2,1)S(1)}, u32[]{:S(2)}, u32[]{:S(2)}) collective-permute-start(bf16[32,3584]{1,0:T(8,128)(2,1)S(1)} %slice.113), channel_id=1, source_target_pairs={{0,6},{1,7},{2,0},{3,1},{4,2},{5,3},{6,4},{7,5},{8,14},{9,15},{10,... | collective-permute-start | bytes 688136 | tf_op jit(solution)/shard_map/ppermute | solution.py:40
  59.8 5.1 %collective-permute-done.5 = bf16[64,3584]{1,0:T(8,128)(2,1)S(1)} collective-permute-done((bf16[64,3584]{1,0:T(8,128)(2,1)S(1)}, bf16[64,3584]{1,0:T(8,128)(2,1)S(1)}, u32[]{:S(2)}, u32[]{:S(2)}) %collective-permute-start.5) | collective-permute-done | bytes 458784 | tf_op jit(solution)/shard_map/ppermute | solution.py:40
  65.0 2.7 %collective-permute-start.8 = (bf16[32,3584]{1,0:T(8,128)(2,1)S(1)}, bf16[32,3584]{1,0:T(8,128)(2,1)S(1)}, u32[]{:S(2)}, u32[]{:S(2)}) collective-permute-start(bf16[32,3584]{1,0:T(8,128)(2,1)S(1)} %slice.115), channel_id=1, source_target_pairs={{0,6},{1,7},{2,0},{3,1},{4,2},{5,3},{6,4},{7,5},{8,14},{9,15},{10,... | collective-permute-start | bytes 688136 | tf_op jit(solution)/shard_map/ppermute | solution.py:40
  67.7 2.0 %collective-permute-done.14 = bf16[64,3584]{1,0:T(8,128)(2,1)S(1)} collective-permute-done((bf16[64,3584]{1,0:T(8,128)(2,1)S(1)}, bf16[64,3584]{1,0:T(8,128)(2,1)S(1)}, u32[]{:S(2)}, u32[]{:S(2)}) %collective-permute-start.14) | collective-permute-done | bytes 458784 | tf_op jit(solution)/shard_map/ppermute | solution.py:50
  72.1 1.7 collective-permute-start.16
  73.9 2.0 %collective-permute-start.4 = (bf16[256,3584]{1,0:T(8,128)(2,1)S(1)}, bf16[256,3584]{1,0:T(8,128)(2,1)S(1)}, u32[]{:S(2)}, u32[]{:S(2)}) collective-permute-start(bf16[256,3584]{1,0:T(8,128)(2,1)S(1)} %get-tuple-element.26), channel_id=1, source_target_pairs={{0,1},{1,0},{2,3},{3,2},{4,5},{5,4},{6,7},{7,6},{8,9},{9,8},{10,11... | collective-permute-start | bytes 5505032 | tf_op jit(solution)/shard_map/ppermute | solution.py:45
  75.9 1.6 collective-permute-start.9
  77.6 6.9 %collective-permute-done.15 = bf16[64,3584]{1,0:T(8,128)(2,1)S(1)} collective-permute-done((bf16[64,3584]{1,0:T(8,128)(2,1)S(1)}, bf16[64,3584]{1,0:T(8,128)(2,1)S(1)}, u32[]{:S(2)}, u32[]{:S(2)}) %collective-permute-start.15) | collective-permute-done | bytes 458784 | tf_op jit(solution)/shard_map/ppermute | solution.py:40
  84.8 2.8 %collective-permute-start.18 = (bf16[32,3584]{1,0:T(8,128)(2,1)S(1)}, bf16[32,3584]{1,0:T(8,128)(2,1)S(1)}, u32[]{:S(2)}, u32[]{:S(2)}) collective-permute-start(bf16[32,3584]{1,0:T(8,128)(2,1)S(1)} %slice.129), channel_id=1, source_target_pairs={{0,6},{1,7},{2,0},{3,1},{4,2},{5,3},{6,4},{7,5},{8,14},{9,15},{10,... | collective-permute-start | bytes 688136 | tf_op jit(solution)/shard_map/ppermute | solution.py:40
  87.7 3.7 %collective-permute-done.17 = bf16[32,3584]{1,0:T(8,128)(2,1)S(1)} collective-permute-done((bf16[32,3584]{1,0:T(8,128)(2,1)S(1)}, bf16[32,3584]{1,0:T(8,128)(2,1)S(1)}, u32[]{:S(2)}, u32[]{:S(2)}) %collective-permute-start.17) | collective-permute-done | bytes 229408 | tf_op jit(solution)/shard_map/ppermute | solution.py:40
  91.4 2.6 %collective-permute-start.19 = (bf16[256,3584]{1,0:T(8,128)(2,1)S(1)}, bf16[256,3584]{1,0:T(8,128)(2,1)S(1)}, u32[]{:S(2)}, u32[]{:S(2)}) collective-permute-start(bf16[256,3584]{1,0:T(8,128)(2,1)S(1)} %constant_dynamic-update-slice_fusion.22), channel_id=1, source_target_pairs={{0,1},{1,0},{2,3},{3,2},{4,5},{5,4},{6,7},{7,6},{8,9},{9,8},{10,11... | collective-permute-start | bytes 5505032 | tf_op jit(solution)/shard_map/ppermute | solution.py:45
  95.2 1.4 copy-done.7
  97.9 1.4 copy-done.2
  106.4 26.1 %collective-permute-done.20 = bf16[3,512,256]{2,1,0:T(8,128)(2,1)S(1)} collective-permute-done((bf16[3,512,256]{2,1,0:T(8,128)(2,1)S(1)}, bf16[3,512,256]{2,1,0:T(8,128)(2,1)S(1)}, u32[]{:S(2)}, u32[]{:S(2)}) %collective-permute-start.20) | collective-permute-done | bytes 786464 | tf_op jit(solution)/shard_map/ppermute | solution.py:50
  132.7 2.2 %fusion.13 = bf16[1,1792,256]{2,1,0:T(8,128)(2,1)} fusion(bf16[256,1792]{1,0:T(8,128)(2,1)S(1)} %get-tuple-element.6, bf16[256,1792]{1,0:T(8,128)(2,1)S(1)} %copy-done.4, bf16[512,1792]{1,0:T(8,128)(2,1)S(1)} %slice_select_fusion.1, bf16[3,1024,256]{2,1,0:T(8,128)(2,1)S(1)} %pad_maximum_fusion.1), kind=kOutput, calls=%fused_computation.21 | convolution fusion | flops 950992896 | bytes 5111808 | tf_op jit(solution)/shard_map/dot_general | solution.py:28
  135.6 3.3 %collective-permute-start.11 = (bf16[64,3584]{1,0:T(8,128)(2,1)S(1)}, bf16[64,3584]{1,0:T(8,128)(2,1)S(1)}, u32[]{:S(2)}, u32[]{:S(2)}) collective-permute-start(bf16[64,3584]{1,0:T(8,128)(2,1)S(1)} %get-tuple-element.8), channel_id=1, source_target_pairs={{0,6},{1,7},{2,0},{3,1},{4,2},{5,3},{6,4},{7,5},{8,14},{9,15},{10,... | collective-permute-start | bytes 1376264 | tf_op jit(solution)/shard_map/ppermute | solution.py:40
  140.2 2.2 %fusion.14 = bf16[1,1792,256]{2,1,0:T(8,128)(2,1)} fusion(bf16[256,1792]{1,0:T(8,128)(2,1)S(1)} %get-tuple-element.6, bf16[256,1792]{1,0:T(8,128)(2,1)S(1)} %copy-done.4, bf16[512,1792]{1,0:T(8,128)(2,1)S(1)} %slice_select_fusion.1, bf16[3,1024,256]{2,1,0:T(8,128)(2,1)S(1)} %pad_maximum_fusion.1), kind=kOutput, calls=%fused_computation.22 | convolution fusion | flops 950992896 | bytes 5111808 | tf_op jit(solution)/shard_map/dot_general | solution.py:28
  142.4 15.6 %collective-permute-done.11 = bf16[64,3584]{1,0:T(8,128)(2,1)S(1)} collective-permute-done((bf16[64,3584]{1,0:T(8,128)(2,1)S(1)}, bf16[64,3584]{1,0:T(8,128)(2,1)S(1)}, u32[]{:S(2)}, u32[]{:S(2)}) %collective-permute-start.11) | collective-permute-done | bytes 458784 | tf_op jit(solution)/shard_map/ppermute | solution.py:40
  158.0 3.2 %collective-permute-done.12 = bf16[64,3584]{1,0:T(8,128)(2,1)S(1)} collective-permute-done((bf16[64,3584]{1,0:T(8,128)(2,1)S(1)}, bf16[64,3584]{1,0:T(8,128)(2,1)S(1)}, u32[]{:S(2)}, u32[]{:S(2)}) %collective-permute-start.12) | collective-permute-done | bytes 458784 | tf_op jit(solution)/shard_map/ppermute | solution.py:40
  162.2 7.7 %all-to-all-start.2 = ((bf16[8,8,3584]{2,1,0:T(8,128)(2,1)}), bf16[8,8,3584]{2,1,0:T(8,128)(2,1)S(1)}, u32[]{:S(2)}, u32[]{:S(2)}) async-start(bf16[8,8,3584]{2,1,0:T(8,128)(2,1)} %fusion.31), calls=%async_computation.2 | async-start | bytes 917504 | tf_op jit(solution)/shard_map/all_to_all | solution.py:56
  170.0 2.6 %fusion.15 = bf16[1,1792,256]{2,1,0:T(8,128)(2,1)S(1)} fusion(bf16[256,1792]{1,0:T(8,128)(2,1)} %get-tuple-element.7, bf16[256,1792]{1,0:T(8,128)(2,1)S(1)} %get-tuple-element.5, bf16[512,1792]{1,0:T(8,128)(2,1)S(1)} %slice_select_fusion, bf16[3,1024,256]{2,1,0:T(8,128)(2,1)} %copy-done.3), kind=kOutput, calls=%fused_computation.23 | convolution fusion | flops 950992896 | bytes 5111808 | tf_op jit(solution)/shard_map/dot_general | solution.py:28
  172.6 1.8 %maximum_bitcast_fusion = bf16[1,3,1792,256]{3,2,1,0:T(8,128)(2,1)} fusion(bf16[1,1792,256]{2,1,0:T(8,128)(2,1)S(1)} %fusion.15, bf16[1,1792,256]{2,1,0:T(8,128)(2,1)S(1)} %copy-done.6, bf16[1,1792,256]{2,1,0:T(8,128)(2,1)S(1)} %copy-done.5), kind=kLoop, calls=%fused_computation.17 | loop fusion | flops 2752512 | bytes 5505024 | tf_op jit(solution)/shard_map/broadcast_in_dim | solution.py:146
  174.5 6.6 %all-to-all-done.2 = bf16[8,8,3584]{2,1,0:T(8,128)(2,1)S(1)} async-done(((bf16[8,8,3584]{2,1,0:T(8,128)(2,1)}), bf16[8,8,3584]{2,1,0:T(8,128)(2,1)S(1)}, u32[]{:S(2)}, u32[]{:S(2)}) %all-to-all-start.2) | async-done | bytes 458784 | tf_op jit(solution)/shard_map/all_to_all | solution.py:56
  181.1 1.4 fusion
  (93 shorter events, 23.1 us)
Async XLA Ops:
  0.6 99.7 %copy-start = (bf16[1,3584,256]{2,1,0:T(8,128)(2,1)S(1)}, bf16[1,3584,256]{2,1,0:T(8,128)(2,1)}, u32[]{:S(2)}) copy-start(bf16[1,3584,256]{2,1,0:T(8,128)(2,1)} %param.12) | copy-start | bytes 5505028
  6.0 27.6 %all-to-all-start = ((bf16[8,8,3584]{2,1,0:T(8,128)(2,1)}), bf16[8,8,3584]{2,1,0:T(8,128)(2,1)S(1)}, u32[]{:S(2)}, u32[]{:S(2)}) async-start(bf16[8,8,3584]{2,1,0:T(8,128)(2,1)} %fusion.2), calls=%async_computation | async-start | bytes 917504 | tf_op jit(solution)/shard_map/all_to_all | solution.py:56
  33.5 18.7 %all-to-all-start.1 = ((bf16[8,8,3584]{2,1,0:T(8,128)(2,1)}), bf16[8,8,3584]{2,1,0:T(8,128)(2,1)S(1)}, u32[]{:S(2)}, u32[]{:S(2)}) async-start(bf16[8,8,3584]{2,1,0:T(8,128)(2,1)} %fusion.3), calls=%async_computation.1 | async-start | bytes 917504 | tf_op jit(solution)/shard_map/all_to_all | solution.py:56
  37.0 18.9 %collective-permute-start = (bf16[64,3584]{1,0:T(8,128)(2,1)S(1)}, bf16[64,3584]{1,0:T(8,128)(2,1)}, u32[]{:S(2)}, u32[]{:S(2)}) collective-permute-start(bf16[64,3584]{1,0:T(8,128)(2,1)S(1)} %bitcast.85), channel_id=1, source_target_pairs={{0,2},{1,3},{2,4},{3,5},{4,6},{5,7},{6,0},{7,1},{8,10},{9,11},{10,... | collective-permute-start | bytes 1376264 | tf_op jit(solution)/shard_map/ppermute | solution.py:40
  38.3 18.7 %collective-permute-start.1 = (bf16[64,3584]{1,0:T(8,128)(2,1)S(1)}, bf16[64,3584]{1,0:T(8,128)(2,1)S(1)}, u32[]{:S(2)}, u32[]{:S(2)}) collective-permute-start(bf16[64,3584]{1,0:T(8,128)(2,1)S(1)} %bitcast.86), channel_id=1, source_target_pairs={{0,6},{1,7},{2,0},{3,1},{4,2},{5,3},{6,4},{7,5},{8,14},{9,15},{10,... | collective-permute-start | bytes 1376264 | tf_op jit(solution)/shard_map/ppermute | solution.py:40
  52.3 12.6 %collective-permute-start.5 = (bf16[64,3584]{1,0:T(8,128)(2,1)S(1)}, bf16[64,3584]{1,0:T(8,128)(2,1)S(1)}, u32[]{:S(2)}, u32[]{:S(2)}) collective-permute-start(bf16[64,3584]{1,0:T(8,128)(2,1)S(1)} %bitcast.82), channel_id=1, source_target_pairs={{0,2},{1,3},{2,4},{3,5},{4,6},{5,7},{6,0},{7,1},{8,10},{9,11},{10,... | collective-permute-start | bytes 1376264 | tf_op jit(solution)/shard_map/ppermute | solution.py:40
  53.5 11.5 %collective-permute-start.6 = (bf16[64,3584]{1,0:T(8,128)(2,1)S(1)}, bf16[64,3584]{1,0:T(8,128)(2,1)S(1)}, u32[]{:S(2)}, u32[]{:S(2)}) collective-permute-start(bf16[64,3584]{1,0:T(8,128)(2,1)S(1)} %bitcast.83), channel_id=1, source_target_pairs={{0,6},{1,7},{2,0},{3,1},{4,2},{5,3},{6,4},{7,5},{8,14},{9,15},{10,... | collective-permute-start | bytes 1376264 | tf_op jit(solution)/shard_map/ppermute | solution.py:40
  55.1 14.6 %collective-permute-start.14 = (bf16[64,3584]{1,0:T(8,128)(2,1)S(1)}, bf16[64,3584]{1,0:T(8,128)(2,1)S(1)}, u32[]{:S(2)}, u32[]{:S(2)}) collective-permute-start(bf16[64,3584]{1,0:T(8,128)(2,1)S(1)} %pad_maximum_fusion.5), channel_id=1, source_target_pairs={{0,192},{64,128},{128,64},{192,0},{1,193},{65,129},{129,65},{193,1... | collective-permute-start | bytes 1376264 | tf_op jit(solution)/shard_map/ppermute | solution.py:50
  56.9 15.2 %collective-permute-start.2 = (bf16[32,3584]{1,0:T(8,128)(2,1)S(1)}, bf16[32,3584]{1,0:T(8,128)(2,1)S(1)}, u32[]{:S(2)}, u32[]{:S(2)}) collective-permute-start(bf16[32,3584]{1,0:T(8,128)(2,1)S(1)} %slice.112), channel_id=1, source_target_pairs={{0,2},{1,3},{2,4},{3,5},{4,6},{5,7},{6,0},{7,1},{8,10},{9,11},{10,... | collective-permute-start | bytes 688136 | tf_op jit(solution)/shard_map/ppermute | solution.py:40
  57.0 16.8 %collective-permute-start.3 = (bf16[32,3584]{1,0:T(8,128)(2,1)S(1)}, bf16[32,3584]{1,0:T(8,128)(2,1)S(1)}, u32[]{:S(2)}, u32[]{:S(2)}) collective-permute-start(bf16[32,3584]{1,0:T(8,128)(2,1)S(1)} %slice.113), channel_id=1, source_target_pairs={{0,6},{1,7},{2,0},{3,1},{4,2},{5,3},{6,4},{7,5},{8,14},{9,15},{10,... | collective-permute-start | bytes 688136 | tf_op jit(solution)/shard_map/ppermute | solution.py:40
  64.9 11.0 %collective-permute-start.7 = (bf16[32,3584]{1,0:T(8,128)(2,1)S(1)}, bf16[32,3584]{1,0:T(8,128)(2,1)S(1)}, u32[]{:S(2)}, u32[]{:S(2)}) collective-permute-start(bf16[32,3584]{1,0:T(8,128)(2,1)S(1)} %slice.114), channel_id=1, source_target_pairs={{0,2},{1,3},{2,4},{3,5},{4,6},{5,7},{6,0},{7,1},{8,10},{9,11},{10,... | collective-permute-start | bytes 688136 | tf_op jit(solution)/shard_map/ppermute | solution.py:40
  65.0 10.9 %collective-permute-start.8 = (bf16[32,3584]{1,0:T(8,128)(2,1)S(1)}, bf16[32,3584]{1,0:T(8,128)(2,1)S(1)}, u32[]{:S(2)}, u32[]{:S(2)}) collective-permute-start(bf16[32,3584]{1,0:T(8,128)(2,1)S(1)} %slice.115), channel_id=1, source_target_pairs={{0,6},{1,7},{2,0},{3,1},{4,2},{5,3},{6,4},{7,5},{8,14},{9,15},{10,... | collective-permute-start | bytes 688136 | tf_op jit(solution)/shard_map/ppermute | solution.py:40
  69.7 14.8 %collective-permute-start.15 = (bf16[64,3584]{1,0:T(8,128)(2,1)S(1)}, bf16[64,3584]{1,0:T(8,128)(2,1)S(1)}, u32[]{:S(2)}, u32[]{:S(2)}) collective-permute-start(bf16[64,3584]{1,0:T(8,128)(2,1)S(1)} %collective-permute-done.14), channel_id=1, source_target_pairs={{0,2},{1,3},{2,4},{3,5},{4,6},{5,7},{6,0},{7,1},{8,10},{9,11},{10,... | collective-permute-start | bytes 1376264 | tf_op jit(solution)/shard_map/ppermute | solution.py:40
  72.1 12.7 %collective-permute-start.16 = (bf16[64,3584]{1,0:T(8,128)(2,1)S(1)}, bf16[64,3584]{1,0:T(8,128)(2,1)S(1)}, u32[]{:S(2)}, u32[]{:S(2)}) collective-permute-start(bf16[64,3584]{1,0:T(8,128)(2,1)S(1)} %collective-permute-done.14), channel_id=1, source_target_pairs={{0,6},{1,7},{2,0},{3,1},{4,2},{5,3},{6,4},{7,5},{8,14},{9,15},{10,... | collective-permute-start | bytes 1376264 | tf_op jit(solution)/shard_map/ppermute | solution.py:40
  73.9 21.2 %collective-permute-start.4 = (bf16[256,3584]{1,0:T(8,128)(2,1)S(1)}, bf16[256,3584]{1,0:T(8,128)(2,1)S(1)}, u32[]{:S(2)}, u32[]{:S(2)}) collective-permute-start(bf16[256,3584]{1,0:T(8,128)(2,1)S(1)} %get-tuple-element.26), channel_id=1, source_target_pairs={{0,1},{1,0},{2,3},{3,2},{4,5},{5,4},{6,7},{7,6},{8,9},{9,8},{10,11... | collective-permute-start | bytes 5505032 | tf_op jit(solution)/shard_map/ppermute | solution.py:45
  75.9 21.8 %collective-permute-start.9 = (bf16[256,3584]{1,0:T(8,128)(2,1)S(1)}, bf16[256,3584]{1,0:T(8,128)(2,1)S(1)}, u32[]{:S(2)}, u32[]{:S(2)}) collective-permute-start(bf16[256,3584]{1,0:T(8,128)(2,1)S(1)} %get-tuple-element.30), channel_id=1, source_target_pairs={{0,1},{1,0},{2,3},{3,2},{4,5},{5,4},{6,7},{7,6},{8,9},{9,8},{10,11... | collective-permute-start | bytes 5505032 | tf_op jit(solution)/shard_map/ppermute | solution.py:45
  84.6 6.8 %collective-permute-start.17 = (bf16[32,3584]{1,0:T(8,128)(2,1)S(1)}, bf16[32,3584]{1,0:T(8,128)(2,1)S(1)}, u32[]{:S(2)}, u32[]{:S(2)}) collective-permute-start(bf16[32,3584]{1,0:T(8,128)(2,1)S(1)} %slice.128), channel_id=1, source_target_pairs={{0,2},{1,3},{2,4},{3,5},{4,6},{5,7},{6,0},{7,1},{8,10},{9,11},{10,... | collective-permute-start | bytes 688136 | tf_op jit(solution)/shard_map/ppermute | solution.py:40
  84.8 6.7 %collective-permute-start.18 = (bf16[32,3584]{1,0:T(8,128)(2,1)S(1)}, bf16[32,3584]{1,0:T(8,128)(2,1)S(1)}, u32[]{:S(2)}, u32[]{:S(2)}) collective-permute-start(bf16[32,3584]{1,0:T(8,128)(2,1)S(1)} %slice.129), channel_id=1, source_target_pairs={{0,6},{1,7},{2,0},{3,1},{4,2},{5,3},{6,4},{7,5},{8,14},{9,15},{10,... | collective-permute-start | bytes 688136 | tf_op jit(solution)/shard_map/ppermute | solution.py:40
  91.4 13.9 %collective-permute-start.19 = (bf16[256,3584]{1,0:T(8,128)(2,1)S(1)}, bf16[256,3584]{1,0:T(8,128)(2,1)S(1)}, u32[]{:S(2)}, u32[]{:S(2)}) collective-permute-start(bf16[256,3584]{1,0:T(8,128)(2,1)S(1)} %constant_dynamic-update-slice_fusion.22), channel_id=1, source_target_pairs={{0,1},{1,0},{2,3},{3,2},{4,5},{5,4},{6,7},{7,6},{8,9},{9,8},{10,11... | collective-permute-start | bytes 5505032 | tf_op jit(solution)/shard_map/ppermute | solution.py:45
  95.1 1.5 copy-start.7
  97.7 1.5 copy-start.2
  104.1 30.8 %collective-permute-start.10 = (bf16[256,3584]{1,0:T(8,128)(2,1)S(1)}, bf16[256,3584]{1,0:T(8,128)(2,1)S(1)}, u32[]{:S(2)}, u32[]{:S(2)}) collective-permute-start(bf16[256,3584]{1,0:T(8,128)(2,1)S(1)} %slice.164), channel_id=1, source_target_pairs={{0,1},{1,0},{2,3},{3,2},{4,5},{5,4},{6,7},{7,6},{8,9},{9,8},{10,11... | collective-permute-start | bytes 5505032 | tf_op jit(solution)/shard_map/ppermute | solution.py:45
  104.5 28.0 %collective-permute-start.20 = (bf16[3,512,256]{2,1,0:T(8,128)(2,1)S(1)}, bf16[3,512,256]{2,1,0:T(8,128)(2,1)S(1)}, u32[]{:S(2)}, u32[]{:S(2)}) collective-permute-start(bf16[3,512,256]{2,1,0:T(8,128)(2,1)S(1)} %pad_maximum_fusion.4), channel_id=1, source_target_pairs={{0,192},{64,128},{128,64},{192,0},{1,193},{65,129},{129,65},{193,1... | collective-permute-start | bytes 2359304 | tf_op jit(solution)/shard_map/ppermute | solution.py:50
  106.4 26.3 %copy-start.4 = (bf16[256,1792]{1,0:T(8,128)(2,1)S(1)}, bf16[256,1792]{1,0:T(8,128)(2,1)}, u32[]{:S(2)}) copy-start(bf16[256,1792]{1,0:T(8,128)(2,1)} %get-tuple-element.4) | copy-start | bytes 2752516
  132.6 7.5 %copy-start.3 = (bf16[3,1024,256]{2,1,0:T(8,128)(2,1)}, bf16[3,1024,256]{2,1,0:T(8,128)(2,1)S(1)}, u32[]{:S(2)}) copy-start(bf16[3,1024,256]{2,1,0:T(8,128)(2,1)S(1)} %pad_maximum_fusion.1) | copy-start | bytes 4718596
  135.6 22.4 %collective-permute-start.11 = (bf16[64,3584]{1,0:T(8,128)(2,1)S(1)}, bf16[64,3584]{1,0:T(8,128)(2,1)S(1)}, u32[]{:S(2)}, u32[]{:S(2)}) collective-permute-start(bf16[64,3584]{1,0:T(8,128)(2,1)S(1)} %get-tuple-element.8), channel_id=1, source_target_pairs={{0,6},{1,7},{2,0},{3,1},{4,2},{5,3},{6,4},{7,5},{8,14},{9,15},{10,... | collective-permute-start | bytes 1376264 | tf_op jit(solution)/shard_map/ppermute | solution.py:40
  138.9 22.3 %collective-permute-start.12 = (bf16[64,3584]{1,0:T(8,128)(2,1)S(1)}, bf16[64,3584]{1,0:T(8,128)(2,1)S(1)}, u32[]{:S(2)}, u32[]{:S(2)}) collective-permute-start(bf16[64,3584]{1,0:T(8,128)(2,1)S(1)} %get-tuple-element.10), channel_id=1, source_target_pairs={{0,2},{1,3},{2,4},{3,5},{4,6},{5,7},{6,0},{7,1},{8,10},{9,11},{10,... | collective-permute-start | bytes 1376264 | tf_op jit(solution)/shard_map/ppermute | solution.py:40
  138.9 22.3 %collective-permute-start.13 = (bf16[64,3584]{1,0:T(8,128)(2,1)S(1)}, bf16[64,3584]{1,0:T(8,128)(2,1)S(1)}, u32[]{:S(2)}, u32[]{:S(2)}) collective-permute-start(bf16[64,3584]{1,0:T(8,128)(2,1)S(1)} %get-tuple-element.9), channel_id=1, source_target_pairs={{0,4},{1,5},{2,6},{3,7},{4,0},{5,1},{6,2},{7,3},{8,12},{9,13},{10,... | collective-permute-start | bytes 1376264 | tf_op jit(solution)/shard_map/ppermute | solution.py:40
  162.2 18.8 %all-to-all-start.2 = ((bf16[8,8,3584]{2,1,0:T(8,128)(2,1)}), bf16[8,8,3584]{2,1,0:T(8,128)(2,1)S(1)}, u32[]{:S(2)}, u32[]{:S(2)}) async-start(bf16[8,8,3584]{2,1,0:T(8,128)(2,1)} %fusion.31), calls=%async_computation.2 | async-start | bytes 917504 | tf_op jit(solution)/shard_map/all_to_all | solution.py:56
  170.0 2.6 %copy-start.5 = (bf16[1,1792,256]{2,1,0:T(8,128)(2,1)S(1)}, bf16[1,1792,256]{2,1,0:T(8,128)(2,1)}, u32[]{:S(2)}) copy-start(bf16[1,1792,256]{2,1,0:T(8,128)(2,1)} %fusion.13) | copy-start | bytes 2752516
  170.0 2.6 %copy-start.6 = (bf16[1,1792,256]{2,1,0:T(8,128)(2,1)S(1)}, bf16[1,1792,256]{2,1,0:T(8,128)(2,1)}, u32[]{:S(2)}) copy-start(bf16[1,1792,256]{2,1,0:T(8,128)(2,1)} %fusion.14) | copy-start | bytes 2752516
  172.6 9.8 %copy-start.1 = (bf16[1,3584,256]{2,1,0:T(8,128)(2,1)S(1)}, bf16[1,3584,256]{2,1,0:T(8,128)(2,1)}, u32[]{:S(2)}) copy-start(bf16[1,3584,256]{2,1,0:T(8,128)(2,1)} %param.12) | copy-start | bytes 5505028

commit v2 on v1

v2 whole, which is shorter than its diff:
```python
import jax
import jax.numpy as jnp
from jax import lax
from jax.experimental import pallas as pl
from jax.experimental.pallas import tpu as pltpu
from jax.sharding import PartitionSpec as P

GROUP = 8
CAP = 8
CORES = 2
CHIPS = GROUP // CORES
BF16 = jnp.bfloat16
F32 = jnp.float32


def dot(left, right, left_dim, right_dim):
    return lax.dot_general(
        left, right, (((left_dim,), (right_dim,)), ((), ())), preferred_element_type=F32
    )


def cost(microseconds):
    return pl.CostEstimate(
        flops=int(microseconds * 1.0e9), transcendentals=0, bytes_accessed=int(microseconds * 1.0e6)
    )


def run(kernel, outs, *operands, scalars=0, limit=8, us=1.0):
    vmem = pl.BlockSpec(memory_space=pltpu.VMEM)
    smem = pl.BlockSpec(memory_space=pltpu.SMEM)
    return pl.pallas_call(
        kernel,
        out_shape=[jax.ShapeDtypeStruct(shape, dtype) for shape, dtype in outs],
        in_specs=[smem] * scalars + [vmem] * (len(operands) - scalars),
        out_specs=[vmem] * len(outs),
        compiler_params=pltpu.CompilerParams(vmem_limit_bytes=limit << 20),
        cost_estimate=cost(us),
    )(*operands)


def route_kernel(upper, tokens, out_grad, probs, ids, x_rows, sent, select):
    count, top = ids.shape
    experts = x_rows.shape[0] // CAP
    ids = ids[...]
    probs = probs[...].astype(F32)
    lane = lax.broadcasted_iota(jnp.int32, (count, experts), 1)
    member = jnp.zeros((count, experts), F32)
    chosen = jnp.zeros((count, experts), F32)
    for k in range(top):
        hit = ids[:, k : k + 1] == lane
        member = jnp.where(hit, 1.0, member)
        chosen = chosen + jnp.where(hit, probs[:, k : k + 1], 0.0)
    row = lax.broadcasted_iota(jnp.int32, (count, count), 0)
    col = lax.broadcasted_iota(jnp.int32, (count, count), 1)
    earlier = jnp.where(col < row, 1.0, 0.0).astype(BF16)
    position = dot(earlier, member.astype(BF16), 1, 0)
    slots = experts * CAP
    expert_of = lax.broadcasted_iota(jnp.int32, (experts, slots), 1) // CAP
    spread = jnp.where(
        expert_of == lax.broadcasted_iota(jnp.int32, (experts, slots), 0), 1.0, 0.0
    ).astype(BF16)
    member = dot(member.astype(BF16), spread, 1, 0)
    position = dot(position.astype(BF16), spread, 1, 0)
    chosen = dot(chosen.astype(BF16), spread, 1, 0)
    slot = (lax.broadcasted_iota(jnp.int32, (count, slots), 1) % CAP).astype(F32)
    picked = (member == 1.0) & (position == slot)
    sel = jnp.where(picked, 1.0, 0.0).astype(BF16)
    weights = jnp.where(picked, chosen, 0.0).astype(BF16)
    weight = dot(weights, jnp.ones((count, 128), BF16), 0, 0)[:, :1]
    select[...] = sel
    x = dot(sel, tokens[...], 0, 0).astype(BF16)
    g = (dot(sel, out_grad[...], 0, 0) * weight).astype(BF16)
    x_rows[...] = x
    half = x.shape[1] // 2
    high = upper[0] == 1
    own_at = pl.ds(pl.multiple_of(upper[0] * slots, slots), slots)
    mirror_at = pl.ds(pl.multiple_of((1 - upper[0]) * slots, slots), slots)
    sent[own_at, :] = g
    sent[mirror_at, :half] = jnp.where(high, x[:, :half], x[:, half:])
    sent[mirror_at, half:] = jnp.where(high, g[:, :half], g[:, half:])


def split_kernel(upper, arrived, g_here, m_here):
    n = g_here.shape[0]
    g_here[...] = arrived[pl.ds(pl.multiple_of(upper[0] * n, n), n), :]
    m_here[...] = arrived[pl.ds(pl.multiple_of((1 - upper[0]) * n, n), n), :]


def pack_kernel(a, b, c, d, out):
    n = a.shape[0]
    for i, piece in enumerate((a, b, c, d)):
        out[i * n : (i + 1) * n, :] = piece[...]


def up_kernel(x_mine, x_other, w_gate, w_up, gate, up):
    n = x_mine.shape[0]
    for i, x in enumerate((x_mine, x_other)):
        at = slice(i * n, (i + 1) * n)
        gate[at, :] = dot(x[...], w_gate[0], 1, 0)
        up[at, :] = dot(x[...], w_up[0], 1, 0)


def back_kernel(g_mine, g_other, w_down, gate, up, acts):
    n = g_mine.shape[0]
    for i, g in enumerate((g_mine, g_other)):
        at = slice(i * n, (i + 1) * n)
        back = dot(g[...], w_down[0], 1, 1)
        v, u = gate[at, :], up[at, :]
        s = jax.nn.sigmoid(v)
        activated = v * s
        acts[0, at, :] = (back * u * s * (1.0 + v * (1.0 - s))).astype(BF16)
        acts[1, at, :] = (back * activated).astype(BF16)
        acts[2, at, :] = (activated * u).astype(BF16)


def row_other_kernel(acts, w_gate, w_up, out):
    n = out.shape[0]
    out[...] = (
        dot(acts[0, n:, :], w_gate[0], 1, 1) + dot(acts[1, n:, :], w_up[0], 1, 1)
    ).astype(BF16)


def row_mine_kernel(acts, w_gate, w_up, arrived, own, near, next_, far):
    n, rows = own.shape[0], arrived.shape[0]
    total = dot(acts[0, :rows, :], w_gate[0], 1, 1) + dot(acts[1, :rows, :], w_up[0], 1, 1)
    total = total + arrived[...].astype(F32)
    for i, out in enumerate((own, near, next_, far)):
        out[...] = total[i * n : (i + 1) * n].astype(out.dtype)


def total_kernel(own, near, next_, far, out):
    out[...] = (
        own[...] + near[...].astype(F32) + next_[...].astype(F32) + far[...].astype(F32)
    ).astype(BF16)


def tokens_kernel(select, rows, out):
    out[...] = dot(select[...], rows[...], 1, 0).astype(BF16)


def weights_kernel(upper, xm, xo, gm, go, mxm, mxo, mgm, mgo, acts, m_acts, out):
    x = jnp.concatenate([xm[...], xo[...], mxm[...], mxo[...]])
    g = jnp.concatenate([gm[...], go[...], mgm[...], mgo[...]])
    for i, rows in enumerate((x, x, g)):
        d = jnp.concatenate([acts[i], m_acts[i]])
        out[0, i] = dot(rows, d, 0, 0).astype(BF16)


def weight_grads_of(upper, x_mine, x_other, g_mine, g_other, m_mine, m_other, *acts):
    rows, features = x_mine.shape
    units = acts[0].shape[2]
    tile = 256
    steps = features // 2 // tile
    kept = pl.BlockSpec((rows, tile), lambda i, s: (0, s[0] * steps + i))
    first = pl.BlockSpec((rows, tile), lambda i, s: (0, i))
    second = pl.BlockSpec((rows, tile), lambda i, s: (0, steps + i))
    whole = pl.BlockSpec(acts[0].shape, lambda i, s: (0, 0, 0))
    return pl.pallas_call(
        weights_kernel,
        out_shape=jax.ShapeDtypeStruct((1, 3, features // 2, units), BF16),
        grid_spec=pltpu.PrefetchScalarGridSpec(
            num_scalar_prefetch=1,
            grid=(steps,),
            in_specs=[kept] * 4 + [first] * 2 + [second] * 2 + [whole] * 2,
            out_specs=pl.BlockSpec((1, 3, tile, units), lambda i, s: (0, 0, i, 0)),
        ),
        compiler_params=pltpu.CompilerParams(vmem_limit_bytes=16 << 20),
        cost_estimate=cost(0.1),
    )(upper, x_mine, x_other, g_mine, g_other, m_mine, m_other, m_mine, m_other, *acts)


def permute_members(value, move):
    width = lax.axis_size("expert")
    pairs = []
    for source in range(width):
        group, member = divmod(source, GROUP)
        chip, core = divmod(member, CORES)
        chip, core = move(chip, core)
        pairs.append((source, group * GROUP + chip % CHIPS * CORES + core))
    return lax.ppermute(value, "expert", pairs)


def outward(value):
    return permute_members(value, lambda chip, core: (chip + 1 - 2 * core, core))


def inward(value):
    return permute_members(value, lambda chip, core: (chip - 1 + 2 * core, core))


def across(value):
    return permute_members(value, lambda chip, core: (chip + 2, core))


def other_core(value):
    return permute_members(value, lambda chip, core: (chip, 1 - core))


def mirror(value):
    count = lax.axis_size("pipe")
    return lax.ppermute(value, "pipe", [(k, count - 1 - k) for k in range(count)])


def across_groups(value):
    width = lax.axis_size("expert")
    groups = [[e * GROUP + g for e in range(width // GROUP)] for g in range(GROUP)]
    return lax.all_to_all(
        value, "expert", split_axis=0, concat_axis=0, axis_index_groups=groups, tiled=True
    )


def after(value, *others):
    return lax.optimization_barrier((value, *others))[0]


def across_sections(value):
    width, count = lax.axis_size("expert"), lax.axis_size("pipe")
    groups = [
        [section * width + e * GROUP + g for section in (k, count - 1 - k) for e in range(width // GROUP)]
        for k in range(count // 2)
        for g in range(GROUP)
    ]
    return lax.all_to_all(
        value, ("pipe", "expert"), split_axis=0, concat_axis=0, axis_index_groups=groups, tiled=True
    )


def pack(*pieces, us=1.0):
    rows, features = pieces[0].shape
    return run(pack_kernel, [((len(pieces) * rows, features), BF16)], *pieces, limit=2, us=us)[0]


def together(*values):
    return lax.optimization_barrier(values)


def body(tokens, out_grad, probs, expert_ids, w_gate, w_up, w_down):
    in_flight = lax.axis_size("expert") // GROUP
    features = tokens.shape[1]
    units = w_gate.shape[2]
    slots = in_flight * CAP
    upper = (lax.axis_index("pipe") >= lax.axis_size("pipe") // 2).astype(jnp.int32)
    upper = upper.reshape(1)
    rows = ((slots, features), BF16)
    x_rows, sent, select = run(
        route_kernel,
        [rows, ((2 * slots, features), BF16), ((tokens.shape[0], slots), BF16)],
        upper,
        tokens,
        out_grad,
        probs,
        expert_ids,
        scalars=1,
    )
    x_here = across_groups(x_rows)
    arrived = across_sections(after(sent, x_here))
    x_near, x_next = together(outward(x_here), inward(x_here))
    x_far = outward(x_near)
    arrived = after(arrived, x_near, x_next, x_far)
    g_here, m_here = run(split_kernel, [rows] * 2, upper, arrived, scalars=1, limit=2)
    x_mine = pack(x_here, x_near, x_next, x_far)
    x_other = other_core(x_mine)
    g_near, g_next, _ = together(outward(g_here), inward(g_here), x_mine)
    g_far = outward(g_near)
    gate_shape = ((2 * x_mine.shape[0], units), F32)
    gate, up = run(up_kernel, [gate_shape] * 2, x_mine, x_other, w_gate, w_up, us=3.0)
    g_far = after(g_far, gate)
    g_mine = pack(g_here, g_near, g_next, g_far)
    g_other = other_core(g_mine)

    m_here = after(m_here, g_far)
    m_near, m_next = outward(m_here), inward(m_here)
    acts_shape = ((3, gate.shape[0], units), BF16)
    acts = run(back_kernel, [acts_shape], g_mine, g_other, w_down, gate, up, us=3.0)[0]
    m_acts = mirror(acts)
    ready, m_near, m_next = together(acts, m_near, m_next)
    part = run(row_other_kernel, [(x_other.shape, BF16)], ready, w_gate, w_up, limit=14)[0]
    part = other_core(part)
    own, near, next_, far = run(
        row_mine_kernel, [(rows[0], F32), rows, rows, rows], ready, w_gate, w_up, part, limit=14
    )
    near, next_, far, m_far = together(
        inward(near), outward(next_), across(far), outward(m_near)
    )
    total = run(total_kernel, [rows], own, near, next_, far)[0]
    m_far, m_acts, _ = together(m_far, m_acts, total)
    m_mine = pack(m_here, m_near, m_next, m_far, us=10.0)
    m_other = other_core(m_mine)
    returned = across_groups(total)
    weight_grads = weight_grads_of(
        upper, x_mine, x_other, g_mine, g_other, m_mine, m_other, acts, m_acts
    )
    returned, weight_grads = together(returned, weight_grads)
    tokens_grad = run(tokens_kernel, [(tokens.shape, BF16)], select, returned)[0]
    return (tokens_grad, weight_grads)


def solution(mesh):
    return jax.shard_map(
        body,
        mesh=mesh,
        in_specs=(
            P(("pipe", "expert"), None),
            P(("pipe", "expert"), None),
            P(("pipe", "expert"), None),
            P(("pipe", "expert"), None),
            P("pipe", None, "expert"),
            P("pipe", None, "expert"),
            P("pipe", "expert", None),
        ),
        out_specs=(P(("pipe", "expert"), None), P("pipe", None, None, "expert")),
        check_vma=False,
    )
```

time: 186 us -> 159 us (0.85)
  waiting for transfers between devices: 97.3 us -> 60.6 us
  blocking collectives: 0 us -> 27.4 us
  Pallas kernels: 0 us -> 19.8 us
  matrix products: 18.9 us -> 0 us
  starting transfers between devices: 50.1 us -> 36.3 us
  other arithmetic: 6.52 us -> 0 us
  local copies, waits for them, and re-layouts: 8.51 us -> 12 us
    all_to_all x3 -> x1, waiting for transfers between devices: 34.5 us -> 0.91 us  [across_groups(): lax.all_to_all(value, 'expert', split_axis=0, concat_axis=0, axis_index_g...]
    all_to_all x0 -> x1, blocking collectives: none -> 27.4 us  [across_groups(): lax.all_to_all(value, 'expert', split_axis=0, concat_axis=0, axis_index_g...]
    ppermute x2 -> x1, waiting for transfers between devices: 28.1 us -> 6.89 us  [mirror(): lax.ppermute(value, 'pipe', [(k, count - 1 - k) for k in range(count)])]
    pallas_call x0 -> x12, Pallas kernels: none -> 19.8 us  [the longest x11 12 us: run(): pl.pallas_call(kernel, out_shape=[jax.ShapeDtypeStruct(shape, dtype) for...]
    dot_general x12 -> x0, matrix products: 18.9 us -> none  [the longest x7 11.8 us: contract(): lax.dot_general(left, right, (((left_dim,), (right_dim,)), ((), ())), pre...]
    ppermute x19 -> x16, waiting for transfers between devices: 34.8 us -> 52.2 us  [permute_members(): return lax.ppermute(value, 'expert', pairs)]
    all_to_all x3 -> x1, starting transfers between devices: 21.1 us -> 4.12 us  [across_groups(): lax.all_to_all(value, 'expert', split_axis=0, concat_axis=0, axis_index_g...]
    unnamed x28 -> x34, local copies, waits for them, and re-layouts: 4.34 us -> 12 us
  transfers between devices with their start and end apart: 24 -> 19, of which waited for: 11 -> 17; matrix products, arithmetic and copies ran while one was open for 12% -> 0% of each run, Pallas kernels for 0% -> 9%
where the time goes in v2:
time: 159 us; the launch traced here: 157 us
  waiting for transfers between devices  60.6 us (38%)
  starting transfers between devices  36.3 us (23%)
  blocking collectives  27.4 us (17%)
  Pallas kernels  19.8 us (12%)
  local copies, waits for them, and re-layouts  12 us (8%)
    ppermute x16, waiting for transfers between devices, permute_members(): return lax.ppermute(value, 'expert', pairs)  52.2 us
    all_to_all x1, blocking collectives, across_groups(): lax.all_to_all(value, 'expert', split_axis=0, concat_axis=0, axis_index_g...  27.4 us
    ppermute x16, starting transfers between devices, permute_members(): return lax.ppermute(value, 'expert', pairs)  27 us
    unnamed x34, local copies, waits for them, and re-layouts  12 us
    pallas_call x11, Pallas kernels, run(): pl.pallas_call(kernel, out_shape=[jax.ShapeDtypeStruct(shape, dtype) for...  12 us
    pallas_call x1, Pallas kernels, weight_grads_of(): pl.pallas_call(weights_kernel, out_shape=jax.ShapeDtypeStruct((1, 3, feat...  7.89 us
    ppermute x1, waiting for transfers between devices, mirror(): lax.ppermute(value, 'pipe', [(k, count - 1 - k) for k in range(count)])  6.89 us
    all_to_all x1, starting transfers between devices, across_groups(): lax.all_to_all(value, 'expert', split_axis=0, concat_axis=0, axis_index_g...  4.12 us
  transfers between devices with their start and end apart: 19, of which 17 were waited for; matrix products, arithmetic and copies ran while one was open for 0% of the time, Pallas kernels for 9%

profile of v2, /device:TPU:33, one launch (start us, length us, event | category | flops | bytes accessed | tf_op | source)
XLA Modules:
  0.0 157.0 jit_solution(2439942645600377209)
XLA Ops:
  4.6 1.9 %shard_map.86 = (bf16[64,3584]{1,0:T(8,128)(2,1)S(1)}, bf16[128,3584]{1,0:T(8,128)(2,1)}, bf16[128,64]{1,0:T(8,128)(2,1)S(1)}) custom-call(s32[1]{0:T(128)} %bitcast.upper, bf16[128,3584]{1,0:T(8,128)(2,1)S(1)} %copy-done.10, bf16[128,3584]{1,0:T(8,128)(2,1)S(1)} %copy-done.11, bf16[128,8]{1,0:T(8,128)(2,1)S(1)} %copy.9.probs, s32[128,8]{1,0:T(8,128)S(1)} %copy.10.ids), custom_call_target="tpu_custom_call" | custom-call | flops 1000000000 | bytes 1000000 | tf_op jit(solution)/shard_map/pallas_call | solution.py:31
  6.5 27.4 %all_to_all.35 = bf16[8,8,3584]{2,1,0:T(8,128)(2,1)S(1)} all-to-all(bf16[8,8,3584]{2,1,0:T(8,128)(2,1)S(1)} %bitcast.12), channel_id=1, replica_groups={{0,8,16,24,32,40,48,56},{1,9,17,25,33,41,49,57},{2,10,18,26,34,42,50,58..., dimensions={0} | all-to-all | bytes 917504 | tf_op jit(solution)/shard_map/all_to_all | solution.py:207
  35.1 1.5 collective-permute-start
  36.6 3.6 %all-to-all-start.1 = ((bf16[16,8,3584]{2,1,0:T(8,128)(2,1)}), bf16[16,8,3584]{2,1,0:T(8,128)(2,1)S(1)}, u32[]{:S(2)}, u32[]{:S(2)}) async-start(bf16[16,8,3584]{2,1,0:T(8,128)(2,1)} %bitcast.3), calls=%async_computation.1 | async-start | bytes 1835008 | tf_op jit(solution)/shard_map/all_to_all | solution.py:223
  40.2 2.7 %collective-permute-done.1.c = bf16[64,3584]{1,0:T(8,128)(2,1)S(1)} collective-permute-done((bf16[64,3584]{1,0:T(8,128)(2,1)S(1)}, bf16[64,3584]{1,0:T(8,128)(2,1)S(1)}, u32[]{:S(2)}, u32[]{:S(2)}) %collective-permute-start.1) | collective-permute-done | bytes 458784 | tf_op jit(solution)/shard_map/ppermute | solution.py:180
  43.7 3.3 %collective-permute-done.b = bf16[64,3584]{1,0:T(8,128)(2,1)S(1)} collective-permute-done((bf16[64,3584]{1,0:T(8,128)(2,1)S(1)}, bf16[64,3584]{1,0:T(8,128)(2,1)S(1)}, u32[]{:S(2)}, u32[]{:S(2)}) %collective-permute-start) | collective-permute-done | bytes 458784 | tf_op jit(solution)/shard_map/ppermute | solution.py:180
  47.0 1.6 %collective-permute-start.2 = (bf16[64,3584]{1,0:T(8,128)(2,1)S(1)}, bf16[64,3584]{1,0:T(8,128)(2,1)S(1)}, u32[]{:S(2)}, u32[]{:S(2)}) collective-permute-start(bf16[64,3584]{1,0:T(8,128)(2,1)S(1)} %collective-permute-done.b), channel_id=1, source_target_pairs={{0,2},{1,7},{2,4},{3,1},{4,6},{5,3},{6,0},{7,5},{8,10},{9,15},{10,... | collective-permute-start | bytes 1376264 | tf_op jit(solution)/shard_map/ppermute | solution.py:180
  49.3 5.3 %collective-permute-done.2.d = bf16[64,3584]{1,0:T(8,128)(2,1)S(1)} collective-permute-done((bf16[64,3584]{1,0:T(8,128)(2,1)S(1)}, bf16[64,3584]{1,0:T(8,128)(2,1)S(1)}, u32[]{:S(2)}, u32[]{:S(2)}) %collective-permute-start.2) | collective-permute-done | bytes 458784 | tf_op jit(solution)/shard_map/ppermute | solution.py:180
  56.7 4.0 %collective-permute-start.6 = (bf16[256,3584]{1,0:T(8,128)(2,1)S(1)}, bf16[256,3584]{1,0:T(8,128)(2,1)}, u32[]{:S(2)}, u32[]{:S(2)}) collective-permute-start(bf16[256,3584]{1,0:T(8,128)(2,1)S(1)} %shard_map.88.x_mine.xm), channel_id=1, source_target_pairs={{0,1},{1,0},{2,3},{3,2},{4,5},{5,4},{6,7},{7,6},{8,9},{9,8},{10,11... | collective-permute-start | bytes 5505032 | tf_op jit(solution)/shard_map/ppermute | solution.py:180
  61.5 2.7 %collective-permute-start.3 = (bf16[64,3584]{1,0:T(8,128)(2,1)S(1)}, bf16[64,3584]{1,0:T(8,128)(2,1)S(1)}, u32[]{:S(2)}, u32[]{:S(2)}) collective-permute-start(bf16[64,3584]{1,0:T(8,128)(2,1)S(1)} %get-tuple-element.39.a), channel_id=1, source_target_pairs={{0,2},{1,7},{2,4},{3,1},{4,6},{5,3},{6,0},{7,5},{8,10},{9,15},{10,... | collective-permute-start | bytes 1376264 | tf_op jit(solution)/shard_map/ppermute | solution.py:180
  64.2 7.1 %collective-permute-done.4.c = bf16[64,3584]{1,0:T(8,128)(2,1)S(1)} collective-permute-done((bf16[64,3584]{1,0:T(8,128)(2,1)S(1)}, bf16[64,3584]{1,0:T(8,128)(2,1)S(1)}, u32[]{:S(2)}, u32[]{:S(2)}) %collective-permute-start.4) | collective-permute-done | bytes 458784 | tf_op jit(solution)/shard_map/ppermute | solution.py:180
  71.2 2.3 %collective-permute-done.3.b = bf16[64,3584]{1,0:T(8,128)(2,1)S(1)} collective-permute-done((bf16[64,3584]{1,0:T(8,128)(2,1)S(1)}, bf16[64,3584]{1,0:T(8,128)(2,1)S(1)}, u32[]{:S(2)}, u32[]{:S(2)}) %collective-permute-start.3) | collective-permute-done | bytes 458784 | tf_op jit(solution)/shard_map/ppermute | solution.py:180
  73.5 3.4 %collective-permute-start.5 = (bf16[64,3584]{1,0:T(8,128)(2,1)S(1)}, bf16[64,3584]{1,0:T(8,128)(2,1)S(1)}, u32[]{:S(2)}, u32[]{:S(2)}) collective-permute-start(bf16[64,3584]{1,0:T(8,128)(2,1)S(1)} %collective-permute-done.3.b), channel_id=1, source_target_pairs={{0,2},{1,7},{2,4},{3,1},{4,6},{5,3},{6,0},{7,5},{8,10},{9,15},{10,... | collective-permute-start | bytes 1376264 | tf_op jit(solution)/shard_map/ppermute | solution.py:180
  77.0 3.5 %shard_map.89 = (f32[512,256]{1,0:T(8,128)S(1)}, f32[512,256]{1,0:T(8,128)S(1)}) custom-call(bf16[256,3584]{1,0:T(8,128)(2,1)S(1)} %shard_map.88.x_mine.xm, bf16[256,3584]{1,0:T(8,128)(2,1)} %collective-permute-done.6.x_other.xo, bf16[1,3584,256]{2,1,0:T(8,128)(2,1)S(1)} %copy-done, bf16[1,3584,256]{2,1,0:T(8,128)(2,1)S(1)} %copy-done.1), custom_call_target="tpu_custom_call" | custom-call | flops 3000000000 | bytes 3000000 | tf_op jit(solution)/shard_map/pallas_call | solution.py:31
  80.5 1.8 %collective-permute-done.5.d = bf16[64,3584]{1,0:T(8,128)(2,1)S(1)} collective-permute-done((bf16[64,3584]{1,0:T(8,128)(2,1)S(1)}, bf16[64,3584]{1,0:T(8,128)(2,1)S(1)}, u32[]{:S(2)}, u32[]{:S(2)}) %collective-permute-start.5) | collective-permute-done | bytes 458784 | tf_op jit(solution)/shard_map/ppermute | solution.py:180
  82.5 3.1 %collective-permute-start.7 = (bf16[256,3584]{1,0:T(8,128)(2,1)S(1)}, bf16[256,3584]{1,0:T(8,128)(2,1)S(1)}, u32[]{:S(2)}, u32[]{:S(2)}) collective-permute-start(bf16[256,3584]{1,0:T(8,128)(2,1)S(1)} %shard_map.90.g_mine.gm), channel_id=1, source_target_pairs={{0,1},{1,0},{2,3},{3,2},{4,5},{5,4},{6,7},{7,6},{8,9},{9,8},{10,11... | collective-permute-start | bytes 5505032 | tf_op jit(solution)/shard_map/ppermute | solution.py:180
  85.6 2.7 %collective-permute-start.8 = (bf16[64,3584]{1,0:T(8,128)(2,1)S(1)}, bf16[64,3584]{1,0:T(8,128)(2,1)S(1)}, u32[]{:S(2)}, u32[]{:S(2)}) collective-permute-start(bf16[64,3584]{1,0:T(8,128)(2,1)S(1)} %get-tuple-element.46.a), channel_id=1, source_target_pairs={{0,2},{1,7},{2,4},{3,1},{4,6},{5,3},{6,0},{7,5},{8,10},{9,15},{10,... | collective-permute-start | bytes 1376264 | tf_op jit(solution)/shard_map/ppermute | solution.py:180
  90.3 6.7 %collective-permute-done.9.c = bf16[64,3584]{1,0:T(8,128)(2,1)S(1)} collective-permute-done((bf16[64,3584]{1,0:T(8,128)(2,1)S(1)}, bf16[64,3584]{1,0:T(8,128)(2,1)S(1)}, u32[]{:S(2)}, u32[]{:S(2)}) %collective-permute-start.9) | collective-permute-done | bytes 458784 | tf_op jit(solution)/shard_map/ppermute | solution.py:180
  99.1 1.9 %collective-permute-start.10 = (bf16[256,3584]{1,0:T(8,128)(2,1)S(1)}, bf16[256,3584]{1,0:T(8,128)(2,1)S(1)}, u32[]{:S(2)}, u32[]{:S(2)}) collective-permute-start(bf16[256,3584]{1,0:T(8,128)(2,1)S(1)} %shard_map.92), channel_id=1, source_target_pairs={{0,1},{1,0},{2,3},{3,2},{4,5},{5,4},{6,7},{7,6},{8,9},{9,8},{10,11... | collective-permute-start | bytes 5505032 | tf_op jit(solution)/shard_map/ppermute | solution.py:180
  101.0 1.5 collective-permute-start.15
  105.6 2.7 %collective-permute-start.12 = (bf16[64,3584]{1,0:T(8,128)(2,1)S(1)}, bf16[64,3584]{1,0:T(8,128)(2,1)S(1)}, u32[]{:S(2)}, u32[]{:S(2)}) collective-permute-start(bf16[64,3584]{1,0:T(8,128)(2,1)S(1)} %get-tuple-element.50), channel_id=1, source_target_pairs={{0,2},{1,7},{2,4},{3,1},{4,6},{5,3},{6,0},{7,5},{8,10},{9,15},{10,... | collective-permute-start | bytes 1376264 | tf_op jit(solution)/shard_map/ppermute | solution.py:180
  108.5 2.5 %collective-permute-done.14.d = bf16[64,3584]{1,0:T(8,128)(2,1)S(1)} collective-permute-done((bf16[64,3584]{1,0:T(8,128)(2,1)S(1)}, bf16[64,3584]{1,0:T(8,128)(2,1)S(1)}, u32[]{:S(2)}, u32[]{:S(2)}) %collective-permute-start.14) | collective-permute-done | bytes 458784 | tf_op jit(solution)/shard_map/ppermute | solution.py:180
  111.0 8.4 %collective-permute-done.11.near = bf16[64,3584]{1,0:T(8,128)(2,1)S(1)} collective-permute-done((bf16[64,3584]{1,0:T(8,128)(2,1)S(1)}, bf16[64,3584]{1,0:T(8,128)(2,1)S(1)}, u32[]{:S(2)}, u32[]{:S(2)}) %collective-permute-start.11) | collective-permute-done | bytes 458784 | tf_op jit(solution)/shard_map/ppermute | solution.py:180
  119.4 1.4 collective-permute-done.12.next_
  120.9 8.6 %collective-permute-done.13.far = bf16[64,3584]{1,0:T(8,128)(2,1)S(1)} collective-permute-done((bf16[64,3584]{1,0:T(8,128)(2,1)S(1)}, bf16[64,3584]{1,0:T(8,128)(2,1)S(1)}, u32[]{:S(2)}, u32[]{:S(2)}) %collective-permute-start.13) | collective-permute-done | bytes 458784 | tf_op jit(solution)/shard_map/ppermute | solution.py:180
  129.7 6.9 %collective-permute-done.15.m_acts = bf16[3,512,256]{2,1,0:T(8,128)(2,1)S(1)} collective-permute-done((bf16[3,512,256]{2,1,0:T(8,128)(2,1)S(1)}, bf16[3,512,256]{2,1,0:T(8,128)(2,1)S(1)}, u32[]{:S(2)}, u32[]{:S(2)}) %collective-permute-start.15) | collective-permute-done | bytes 786464 | tf_op jit(solution)/shard_map/ppermute | solution.py:201
  137.2 4.1 %all-to-all-start.2 = ((bf16[8,8,3584]{2,1,0:T(8,128)(2,1)}), bf16[8,8,3584]{2,1,0:T(8,128)(2,1)}, u32[]{:S(2)}, u32[]{:S(2)}) async-start(bf16[8,8,3584]{2,1,0:T(8,128)(2,1)} %bitcast.8), calls=%async_computation.2 | async-start | bytes 917504 | tf_op jit(solution)/shard_map/all_to_all | solution.py:207
  141.4 1.5 copy-done.3
  142.9 1.5 copy-done.5
  144.4 1.5 copy-done.7
  145.9 7.9 %shard_map.96 = bf16[1,3,1792,256]{3,2,1,0:T(8,128)(2,1)} custom-call(s32[1]{0:T(128)} %bitcast.upper, bf16[256,3584]{1,0:T(8,128)(2,1)S(1)} %copy-done.3, bf16[256,3584]{1,0:T(8,128)(2,1)} %collective-permute-done.6.x_other.xo, bf16[256,3584]{1,0:T(8,128)(2,1)S(1)} %copy-done.5, bf16[256,3584]{1,0:T(8,128)(2,1)S(1)} %copy-done.7, ...), custom_call_target="tpu_custom_call" | custom-call | flops 100000000 | bytes 100000 | tf_op jit(solution)/shard_map/pallas_call | solution.py:158
  154.7 2.3 %shard_map.97 = bf16[128,3584]{1,0:T(8,128)(2,1)} custom-call(bf16[128,64]{1,0:T(8,128)(2,1)S(1)} %get-tuple-element.32.select, bf16[64,3584]{1,0:T(8,128)(2,1)} %bitcast.6.rows), custom_call_target="tpu_custom_call" | custom-call | flops 1000000000 | bytes 1000000 | tf_op jit(solution)/shard_map/pallas_call | solution.py:31
  (53 shorter events, 18.9 us)
Async XLA Ops:
  2.2 1.2 copy-start.10
  3.4 1.2 copy-start.11
  33.9 9.0 %collective-permute-start.1 = (bf16[64,3584]{1,0:T(8,128)(2,1)S(1)}, bf16[64,3584]{1,0:T(8,128)(2,1)S(1)}, u32[]{:S(2)}, u32[]{:S(2)}) collective-permute-start(bf16[64,3584]{1,0:T(8,128)(2,1)S(1)} %bitcast.9), channel_id=1, source_target_pairs={{0,6},{1,3},{2,0},{3,5},{4,2},{5,7},{6,4},{7,1},{8,14},{9,11},{10,... | collective-permute-start | bytes 1376264 | tf_op jit(solution)/shard_map/ppermute | solution.py:180
  35.1 11.8 %collective-permute-start = (bf16[64,3584]{1,0:T(8,128)(2,1)S(1)}, bf16[64,3584]{1,0:T(8,128)(2,1)S(1)}, u32[]{:S(2)}, u32[]{:S(2)}) collective-permute-start(bf16[64,3584]{1,0:T(8,128)(2,1)S(1)} %bitcast.10), channel_id=1, source_target_pairs={{0,2},{1,7},{2,4},{3,1},{4,6},{5,3},{6,0},{7,5},{8,10},{9,15},{10,... | collective-permute-start | bytes 1376264 | tf_op jit(solution)/shard_map/ppermute | solution.py:180
  36.6 24.8 %all-to-all-start.1 = ((bf16[16,8,3584]{2,1,0:T(8,128)(2,1)}), bf16[16,8,3584]{2,1,0:T(8,128)(2,1)S(1)}, u32[]{:S(2)}, u32[]{:S(2)}) async-start(bf16[16,8,3584]{2,1,0:T(8,128)(2,1)} %bitcast.3), calls=%async_computation.1 | async-start | bytes 1835008 | tf_op jit(solution)/shard_map/all_to_all | solution.py:223
  47.0 7.6 %collective-permute-start.2 = (bf16[64,3584]{1,0:T(8,128)(2,1)S(1)}, bf16[64,3584]{1,0:T(8,128)(2,1)S(1)}, u32[]{:S(2)}, u32[]{:S(2)}) collective-permute-start(bf16[64,3584]{1,0:T(8,128)(2,1)S(1)} %collective-permute-done.b), channel_id=1, source_target_pairs={{0,2},{1,7},{2,4},{3,1},{4,6},{5,3},{6,0},{7,5},{8,10},{9,15},{10,... | collective-permute-start | bytes 1376264 | tf_op jit(solution)/shard_map/ppermute | solution.py:180
  54.6 1.0 copy-start.13
  56.7 20.2 %copy-start.2 = (bf16[256,3584]{1,0:T(8,128)(2,1)}, bf16[256,3584]{1,0:T(8,128)(2,1)S(1)}, u32[]{:S(2)}) copy-start(bf16[256,3584]{1,0:T(8,128)(2,1)S(1)} %shard_map.88.x_mine.xm) | copy-start | bytes 5505028
  56.7 20.2 %collective-permute-start.6 = (bf16[256,3584]{1,0:T(8,128)(2,1)S(1)}, bf16[256,3584]{1,0:T(8,128)(2,1)}, u32[]{:S(2)}, u32[]{:S(2)}) collective-permute-start(bf16[256,3584]{1,0:T(8,128)(2,1)S(1)} %shard_map.88.x_mine.xm), channel_id=1, source_target_pairs={{0,1},{1,0},{2,3},{3,2},{4,5},{5,4},{6,7},{7,6},{8,9},{9,8},{10,11... | collective-permute-start | bytes 5505032 | tf_op jit(solution)/shard_map/ppermute | solution.py:180
  61.4 15.6 %copy-start = (bf16[1,3584,256]{2,1,0:T(8,128)(2,1)S(1)}, bf16[1,3584,256]{2,1,0:T(8,128)(2,1)}, u32[]{:S(2)}) copy-start(bf16[1,3584,256]{2,1,0:T(8,128)(2,1)} %w_gate.5) | copy-start | bytes 5505028
  61.4 15.6 %copy-start.1 = (bf16[1,3584,256]{2,1,0:T(8,128)(2,1)S(1)}, bf16[1,3584,256]{2,1,0:T(8,128)(2,1)}, u32[]{:S(2)}) copy-start(bf16[1,3584,256]{2,1,0:T(8,128)(2,1)} %w_up.5) | copy-start | bytes 5505028
  61.4 9.8 %collective-permute-start.4 = (bf16[64,3584]{1,0:T(8,128)(2,1)S(1)}, bf16[64,3584]{1,0:T(8,128)(2,1)S(1)}, u32[]{:S(2)}, u32[]{:S(2)}) collective-permute-start(bf16[64,3584]{1,0:T(8,128)(2,1)S(1)} %get-tuple-element.39.a), channel_id=1, source_target_pairs={{0,6},{1,3},{2,0},{3,5},{4,2},{5,7},{6,4},{7,1},{8,14},{9,11},{10,... | collective-permute-start | bytes 1376264 | tf_op jit(solution)/shard_map/ppermute | solution.py:180
  61.5 12.0 %collective-permute-start.3 = (bf16[64,3584]{1,0:T(8,128)(2,1)S(1)}, bf16[64,3584]{1,0:T(8,128)(2,1)S(1)}, u32[]{:S(2)}, u32[]{:S(2)}) collective-permute-start(bf16[64,3584]{1,0:T(8,128)(2,1)S(1)} %get-tuple-element.39.a), channel_id=1, source_target_pairs={{0,2},{1,7},{2,4},{3,1},{4,6},{5,3},{6,0},{7,5},{8,10},{9,15},{10,... | collective-permute-start | bytes 1376264 | tf_op jit(solution)/shard_map/ppermute | solution.py:180
  73.5 8.8 %collective-permute-start.5 = (bf16[64,3584]{1,0:T(8,128)(2,1)S(1)}, bf16[64,3584]{1,0:T(8,128)(2,1)S(1)}, u32[]{:S(2)}, u32[]{:S(2)}) collective-permute-start(bf16[64,3584]{1,0:T(8,128)(2,1)S(1)} %collective-permute-done.3.b), channel_id=1, source_target_pairs={{0,2},{1,7},{2,4},{3,1},{4,6},{5,3},{6,0},{7,5},{8,10},{9,15},{10,... | collective-permute-start | bytes 1376264 | tf_op jit(solution)/shard_map/ppermute | solution.py:180
  82.4 6.6 %copy-start.9 = (bf16[1,256,3584]{2,1,0:T(8,128)(2,1)S(1)}, bf16[1,256,3584]{2,1,0:T(8,128)(2,1)}, u32[]{:S(2)}) copy-start(bf16[1,256,3584]{2,1,0:T(8,128)(2,1)} %w_down.1) | copy-start | bytes 5505028
  82.5 7.8 %copy-start.4 = (bf16[256,3584]{1,0:T(8,128)(2,1)}, bf16[256,3584]{1,0:T(8,128)(2,1)S(1)}, u32[]{:S(2)}) copy-start(bf16[256,3584]{1,0:T(8,128)(2,1)S(1)} %shard_map.90.g_mine.gm) | copy-start | bytes 5505028
  82.5 6.5 %collective-permute-start.7 = (bf16[256,3584]{1,0:T(8,128)(2,1)S(1)}, bf16[256,3584]{1,0:T(8,128)(2,1)S(1)}, u32[]{:S(2)}, u32[]{:S(2)}) collective-permute-start(bf16[256,3584]{1,0:T(8,128)(2,1)S(1)} %shard_map.90.g_mine.gm), channel_id=1, source_target_pairs={{0,1},{1,0},{2,3},{3,2},{4,5},{5,4},{6,7},{7,6},{8,9},{9,8},{10,11... | collective-permute-start | bytes 5505032 | tf_op jit(solution)/shard_map/ppermute | solution.py:180
  85.6 11.4 %collective-permute-start.9 = (bf16[64,3584]{1,0:T(8,128)(2,1)S(1)}, bf16[64,3584]{1,0:T(8,128)(2,1)S(1)}, u32[]{:S(2)}, u32[]{:S(2)}) collective-permute-start(bf16[64,3584]{1,0:T(8,128)(2,1)S(1)} %get-tuple-element.46.a), channel_id=1, source_target_pairs={{0,6},{1,3},{2,0},{3,5},{4,2},{5,7},{6,4},{7,1},{8,14},{9,11},{10,... | collective-permute-start | bytes 1376264 | tf_op jit(solution)/shard_map/ppermute | solution.py:180
  85.6 12.4 %collective-permute-start.8 = (bf16[64,3584]{1,0:T(8,128)(2,1)S(1)}, bf16[64,3584]{1,0:T(8,128)(2,1)S(1)}, u32[]{:S(2)}, u32[]{:S(2)}) collective-permute-start(bf16[64,3584]{1,0:T(8,128)(2,1)S(1)} %get-tuple-element.46.a), channel_id=1, source_target_pairs={{0,2},{1,7},{2,4},{3,1},{4,6},{5,3},{6,0},{7,5},{8,10},{9,15},{10,... | collective-permute-start | bytes 1376264 | tf_op jit(solution)/shard_map/ppermute | solution.py:180
  89.0 1.3 copy-start.6
  99.1 5.3 %collective-permute-start.10 = (bf16[256,3584]{1,0:T(8,128)(2,1)S(1)}, bf16[256,3584]{1,0:T(8,128)(2,1)S(1)}, u32[]{:S(2)}, u32[]{:S(2)}) collective-permute-start(bf16[256,3584]{1,0:T(8,128)(2,1)S(1)} %shard_map.92), channel_id=1, source_target_pairs={{0,1},{1,0},{2,3},{3,2},{4,5},{5,4},{6,7},{7,6},{8,9},{9,8},{10,11... | collective-permute-start | bytes 5505032 | tf_op jit(solution)/shard_map/ppermute | solution.py:180
  101.0 35.6 %collective-permute-start.15 = (bf16[3,512,256]{2,1,0:T(8,128)(2,1)S(1)}, bf16[3,512,256]{2,1,0:T(8,128)(2,1)S(1)}, u32[]{:S(2)}, u32[]{:S(2)}) collective-permute-start(bf16[3,512,256]{2,1,0:T(8,128)(2,1)S(1)} %shard_map.91.acts), channel_id=1, source_target_pairs={{0,192},{64,128},{128,64},{192,0},{1,193},{65,129},{129,65},{193,1... | collective-permute-start | bytes 2359304 | tf_op jit(solution)/shard_map/ppermute | solution.py:201
  102.5 8.5 %collective-permute-start.14 = (bf16[64,3584]{1,0:T(8,128)(2,1)S(1)}, bf16[64,3584]{1,0:T(8,128)(2,1)S(1)}, u32[]{:S(2)}, u32[]{:S(2)}) collective-permute-start(bf16[64,3584]{1,0:T(8,128)(2,1)S(1)} %collective-permute-done.8.b), channel_id=1, source_target_pairs={{0,2},{1,7},{2,4},{3,1},{4,6},{5,3},{6,0},{7,5},{8,10},{9,15},{10,... | collective-permute-start | bytes 1376264 | tf_op jit(solution)/shard_map/ppermute | solution.py:180
  105.5 13.9 %collective-permute-start.11 = (bf16[64,3584]{1,0:T(8,128)(2,1)S(1)}, bf16[64,3584]{1,0:T(8,128)(2,1)S(1)}, u32[]{:S(2)}, u32[]{:S(2)}) collective-permute-start(bf16[64,3584]{1,0:T(8,128)(2,1)S(1)} %get-tuple-element.49), channel_id=1, source_target_pairs={{0,6},{1,3},{2,0},{3,5},{4,2},{5,7},{6,4},{7,1},{8,14},{9,11},{10,... | collective-permute-start | bytes 1376264 | tf_op jit(solution)/shard_map/ppermute | solution.py:180
  105.6 15.2 %collective-permute-start.12 = (bf16[64,3584]{1,0:T(8,128)(2,1)S(1)}, bf16[64,3584]{1,0:T(8,128)(2,1)S(1)}, u32[]{:S(2)}, u32[]{:S(2)}) collective-permute-start(bf16[64,3584]{1,0:T(8,128)(2,1)S(1)} %get-tuple-element.50), channel_id=1, source_target_pairs={{0,2},{1,7},{2,4},{3,1},{4,6},{5,3},{6,0},{7,5},{8,10},{9,15},{10,... | collective-permute-start | bytes 1376264 | tf_op jit(solution)/shard_map/ppermute | solution.py:180
  108.3 21.2 %collective-permute-start.13 = (bf16[64,3584]{1,0:T(8,128)(2,1)S(1)}, bf16[64,3584]{1,0:T(8,128)(2,1)S(1)}, u32[]{:S(2)}, u32[]{:S(2)}) collective-permute-start(bf16[64,3584]{1,0:T(8,128)(2,1)S(1)} %get-tuple-element.51), channel_id=1, source_target_pairs={{0,4},{1,5},{2,6},{3,7},{4,0},{5,1},{6,2},{7,3},{8,12},{9,13},{10,... | collective-permute-start | bytes 1376264 | tf_op jit(solution)/shard_map/ppermute | solution.py:180
  129.7 7.0 %copy-start.8 = (bf16[64,3584]{1,0:T(8,128)(2,1)}, bf16[64,3584]{1,0:T(8,128)(2,1)S(1)}, u32[]{:S(2)}) copy-start(bf16[64,3584]{1,0:T(8,128)(2,1)S(1)} %shard_map.94) | copy-start | bytes 1376260
  136.7 4.7 %collective-permute-start.16 = (bf16[256,3584]{1,0:T(8,128)(2,1)S(1)}, bf16[256,3584]{1,0:T(8,128)(2,1)}, u32[]{:S(2)}, u32[]{:S(2)}) collective-permute-start(bf16[256,3584]{1,0:T(8,128)(2,1)S(1)} %shard_map.95.mxm.mgm), channel_id=1, source_target_pairs={{0,1},{1,0},{2,3},{3,2},{4,5},{5,4},{6,7},{7,6},{8,9},{9,8},{10,11... | collective-permute-start | bytes 5505032 | tf_op jit(solution)/shard_map/ppermute | solution.py:180
  137.2 17.4 %all-to-all-start.2 = ((bf16[8,8,3584]{2,1,0:T(8,128)(2,1)}), bf16[8,8,3584]{2,1,0:T(8,128)(2,1)}, u32[]{:S(2)}, u32[]{:S(2)}) async-start(bf16[8,8,3584]{2,1,0:T(8,128)(2,1)} %bitcast.8), calls=%async_computation.2 | async-start | bytes 917504 | tf_op jit(solution)/shard_map/all_to_all | solution.py:207
  141.4 1.5 copy-start.3
  142.9 1.5 copy-start.5
  144.4 1.5 copy-start.7
  (3 other events, 2.6 us)

commit v3 on v2

--- a/solution.py
+++ b/solution.py
@@ -273,7 +273,7 @@
     acts_shape = ((3, gate.shape[0], units), BF16)
     acts = run(back_kernel, [acts_shape], g_mine, g_other, w_down, gate, up, us=3.0)[0]
     m_acts = mirror(acts)
-    ready, m_near, m_next = together(acts, m_near, m_next)
+    ready, m_near = together(acts, m_near)
     part = run(row_other_kernel, [(x_other.shape, BF16)], ready, w_gate, w_up, limit=14)[0]
     part = other_core(part)
     own, near, next_, far = run(
@@ -283,7 +283,7 @@
         inward(near), outward(next_), across(far), outward(m_near)
     )
     total = run(total_kernel, [rows], own, near, next_, far)[0]
-    m_far, m_acts, _ = together(m_far, m_acts, total)
+    m_far, m_next, m_acts, _ = together(m_far, m_next, m_acts, total)
     m_mine = pack(m_here, m_near, m_next, m_far, us=10.0)
     m_other = other_core(m_mine)
     returned = across_groups(total)

time: 159 us -> 157 us (0.987)
    ppermute x1, waiting for transfers between devices: 6.89 us -> 1.77 us  [mirror(): lax.ppermute(value, 'pipe', [(k, count - 1 - k) for k in range(count)])]
    all_to_all x1, waiting for transfers between devices: 0.91 us -> 3.39 us  [across_groups(): lax.all_to_all(value, 'expert', split_axis=0, concat_axis=0, axis_index_g...]
    ppermute x16, waiting for transfers between devices: 52.2 us -> 54.7 us  [permute_members(): return lax.ppermute(value, 'expert', pairs)]
    ppermute x16, starting transfers between devices: 27 us -> 25.3 us  [permute_members(): return lax.ppermute(value, 'expert', pairs)]
where the time goes in v3:
time: 157 us; the launch traced here: 156 us
  waiting for transfers between devices  60.4 us (38%)
  starting transfers between devices  35.3 us (22%)
  blocking collectives  27.4 us (17%)
  Pallas kernels  19.8 us (13%)
  local copies, waits for them, and re-layouts  12 us (8%)
    ppermute x16, waiting for transfers between devices, permute_members(): return lax.ppermute(value, 'expert', pairs)  54.7 us
    all_to_all x1, blocking collectives, across_groups(): lax.all_to_all(value, 'expert', split_axis=0, concat_axis=0, axis_index_g...  27.4 us
    ppermute x16, starting transfers between devices, permute_members(): return lax.ppermute(value, 'expert', pairs)  25.3 us
    unnamed x34, local copies, waits for them, and re-layouts  12 us
    pallas_call x11, Pallas kernels, run(): pl.pallas_call(kernel, out_shape=[jax.ShapeDtypeStruct(shape, dtype) for...  12 us
    pallas_call x1, Pallas kernels, weight_grads_of(): pl.pallas_call(weights_kernel, out_shape=jax.ShapeDtypeStruct((1, 3, feat...  7.88 us
    all_to_all x1, starting transfers between devices, across_groups(): lax.all_to_all(value, 'expert', split_axis=0, concat_axis=0, axis_index_g...  4.87 us
    all_to_all x1, starting transfers between devices, across_sections(): lax.all_to_all(value, ('pipe', 'expert'), split_axis=0, concat_axis=0, ax...  3.63 us
  transfers between devices with their start and end apart: 19, of which 17 were waited for; matrix products, arithmetic and copies ran while one was open for 0% of the time, Pallas kernels for 9%

profile of v3, /device:TPU:33, one launch (start us, length us, event | category | flops | bytes accessed | tf_op | source)
XLA Modules:
  0.0 155.8 jit_solution(17551274456550474393)
XLA Ops:
  4.6 1.9 %shard_map.86 = (bf16[64,3584]{1,0:T(8,128)(2,1)S(1)}, bf16[128,3584]{1,0:T(8,128)(2,1)}, bf16[128,64]{1,0:T(8,128)(2,1)S(1)}) custom-call(s32[1]{0:T(128)} %bitcast.upper, bf16[128,3584]{1,0:T(8,128)(2,1)S(1)} %copy-done.10, bf16[128,3584]{1,0:T(8,128)(2,1)S(1)} %copy-done.11, bf16[128,8]{1,0:T(8,128)(2,1)S(1)} %copy.9.probs, s32[128,8]{1,0:T(8,128)S(1)} %copy.10.ids), custom_call_target="tpu_custom_call" | custom-call | flops 1000000000 | bytes 1000000 | tf_op jit(solution)/shard_map/pallas_call | solution.py:31
  6.5 27.4 %all_to_all.35 = bf16[8,8,3584]{2,1,0:T(8,128)(2,1)S(1)} all-to-all(bf16[8,8,3584]{2,1,0:T(8,128)(2,1)S(1)} %bitcast.12), channel_id=1, replica_groups={{0,8,16,24,32,40,48,56},{1,9,17,25,33,41,49,57},{2,10,18,26,34,42,50,58..., dimensions={0} | all-to-all | bytes 917504 | tf_op jit(solution)/shard_map/all_to_all | solution.py:207
  35.1 1.5 collective-permute-start
  36.6 3.6 %all-to-all-start.1 = ((bf16[16,8,3584]{2,1,0:T(8,128)(2,1)}), bf16[16,8,3584]{2,1,0:T(8,128)(2,1)S(1)}, u32[]{:S(2)}, u32[]{:S(2)}) async-start(bf16[16,8,3584]{2,1,0:T(8,128)(2,1)} %bitcast.3), calls=%async_computation.1 | async-start | bytes 1835008 | tf_op jit(solution)/shard_map/all_to_all | solution.py:223
  40.2 2.7 %collective-permute-done.1.c = bf16[64,3584]{1,0:T(8,128)(2,1)S(1)} collective-permute-done((bf16[64,3584]{1,0:T(8,128)(2,1)S(1)}, bf16[64,3584]{1,0:T(8,128)(2,1)S(1)}, u32[]{:S(2)}, u32[]{:S(2)}) %collective-permute-start.1) | collective-permute-done | bytes 458784 | tf_op jit(solution)/shard_map/ppermute | solution.py:180
  43.7 3.3 %collective-permute-done.b = bf16[64,3584]{1,0:T(8,128)(2,1)S(1)} collective-permute-done((bf16[64,3584]{1,0:T(8,128)(2,1)S(1)}, bf16[64,3584]{1,0:T(8,128)(2,1)S(1)}, u32[]{:S(2)}, u32[]{:S(2)}) %collective-permute-start) | collective-permute-done | bytes 458784 | tf_op jit(solution)/shard_map/ppermute | solution.py:180
  47.0 1.6 %collective-permute-start.2 = (bf16[64,3584]{1,0:T(8,128)(2,1)S(1)}, bf16[64,3584]{1,0:T(8,128)(2,1)S(1)}, u32[]{:S(2)}, u32[]{:S(2)}) collective-permute-start(bf16[64,3584]{1,0:T(8,128)(2,1)S(1)} %collective-permute-done.b), channel_id=1, source_target_pairs={{0,2},{1,7},{2,4},{3,1},{4,6},{5,3},{6,0},{7,5},{8,10},{9,15},{10,... | collective-permute-start | bytes 1376264 | tf_op jit(solution)/shard_map/ppermute | solution.py:180
  49.3 5.3 %collective-permute-done.2.d = bf16[64,3584]{1,0:T(8,128)(2,1)S(1)} collective-permute-done((bf16[64,3584]{1,0:T(8,128)(2,1)S(1)}, bf16[64,3584]{1,0:T(8,128)(2,1)S(1)}, u32[]{:S(2)}, u32[]{:S(2)}) %collective-permute-start.2) | collective-permute-done | bytes 458784 | tf_op jit(solution)/shard_map/ppermute | solution.py:180
  56.7 4.0 %collective-permute-start.6 = (bf16[256,3584]{1,0:T(8,128)(2,1)S(1)}, bf16[256,3584]{1,0:T(8,128)(2,1)}, u32[]{:S(2)}, u32[]{:S(2)}) collective-permute-start(bf16[256,3584]{1,0:T(8,128)(2,1)S(1)} %shard_map.88.x_mine.xm), channel_id=1, source_target_pairs={{0,1},{1,0},{2,3},{3,2},{4,5},{5,4},{6,7},{7,6},{8,9},{9,8},{10,11... | collective-permute-start | bytes 5505032 | tf_op jit(solution)/shard_map/ppermute | solution.py:180
  61.5 2.7 %collective-permute-start.3 = (bf16[64,3584]{1,0:T(8,128)(2,1)S(1)}, bf16[64,3584]{1,0:T(8,128)(2,1)S(1)}, u32[]{:S(2)}, u32[]{:S(2)}) collective-permute-start(bf16[64,3584]{1,0:T(8,128)(2,1)S(1)} %get-tuple-element.39.a), channel_id=1, source_target_pairs={{0,2},{1,7},{2,4},{3,1},{4,6},{5,3},{6,0},{7,5},{8,10},{9,15},{10,... | collective-permute-start | bytes 1376264 | tf_op jit(solution)/shard_map/ppermute | solution.py:180
  64.2 7.1 %collective-permute-done.4.c = bf16[64,3584]{1,0:T(8,128)(2,1)S(1)} collective-permute-done((bf16[64,3584]{1,0:T(8,128)(2,1)S(1)}, bf16[64,3584]{1,0:T(8,128)(2,1)S(1)}, u32[]{:S(2)}, u32[]{:S(2)}) %collective-permute-start.4) | collective-permute-done | bytes 458784 | tf_op jit(solution)/shard_map/ppermute | solution.py:180
  71.2 2.3 %collective-permute-done.3.b = bf16[64,3584]{1,0:T(8,128)(2,1)S(1)} collective-permute-done((bf16[64,3584]{1,0:T(8,128)(2,1)S(1)}, bf16[64,3584]{1,0:T(8,128)(2,1)S(1)}, u32[]{:S(2)}, u32[]{:S(2)}) %collective-permute-start.3) | collective-permute-done | bytes 458784 | tf_op jit(solution)/shard_map/ppermute | solution.py:180
  73.5 3.4 %collective-permute-start.5 = (bf16[64,3584]{1,0:T(8,128)(2,1)S(1)}, bf16[64,3584]{1,0:T(8,128)(2,1)S(1)}, u32[]{:S(2)}, u32[]{:S(2)}) collective-permute-start(bf16[64,3584]{1,0:T(8,128)(2,1)S(1)} %collective-permute-done.3.b), channel_id=1, source_target_pairs={{0,2},{1,7},{2,4},{3,1},{4,6},{5,3},{6,0},{7,5},{8,10},{9,15},{10,... | collective-permute-start | bytes 1376264 | tf_op jit(solution)/shard_map/ppermute | solution.py:180
  77.0 3.5 %shard_map.89 = (f32[512,256]{1,0:T(8,128)S(1)}, f32[512,256]{1,0:T(8,128)S(1)}) custom-call(bf16[256,3584]{1,0:T(8,128)(2,1)S(1)} %shard_map.88.x_mine.xm, bf16[256,3584]{1,0:T(8,128)(2,1)} %collective-permute-done.6.x_other.xo, bf16[1,3584,256]{2,1,0:T(8,128)(2,1)S(1)} %copy-done, bf16[1,3584,256]{2,1,0:T(8,128)(2,1)S(1)} %copy-done.1), custom_call_target="tpu_custom_call" | custom-call | flops 3000000000 | bytes 3000000 | tf_op jit(solution)/shard_map/pallas_call | solution.py:31
  80.5 1.8 %collective-permute-done.5.d = bf16[64,3584]{1,0:T(8,128)(2,1)S(1)} collective-permute-done((bf16[64,3584]{1,0:T(8,128)(2,1)S(1)}, bf16[64,3584]{1,0:T(8,128)(2,1)S(1)}, u32[]{:S(2)}, u32[]{:S(2)}) %collective-permute-start.5) | collective-permute-done | bytes 458784 | tf_op jit(solution)/shard_map/ppermute | solution.py:180
  82.5 3.1 %collective-permute-start.7 = (bf16[256,3584]{1,0:T(8,128)(2,1)S(1)}, bf16[256,3584]{1,0:T(8,128)(2,1)S(1)}, u32[]{:S(2)}, u32[]{:S(2)}) collective-permute-start(bf16[256,3584]{1,0:T(8,128)(2,1)S(1)} %shard_map.90.g_mine.gm), channel_id=1, source_target_pairs={{0,1},{1,0},{2,3},{3,2},{4,5},{5,4},{6,7},{7,6},{8,9},{9,8},{10,11... | collective-permute-start | bytes 5505032 | tf_op jit(solution)/shard_map/ppermute | solution.py:180
  87.0 1.9 %collective-permute-done.7.g_other.go = bf16[256,3584]{1,0:T(8,128)(2,1)S(1)} collective-permute-done((bf16[256,3584]{1,0:T(8,128)(2,1)S(1)}, bf16[256,3584]{1,0:T(8,128)(2,1)S(1)}, u32[]{:S(2)}, u32[]{:S(2)}) %collective-permute-start.7) | collective-permute-done | bytes 1835040 | tf_op jit(solution)/shard_map/ppermute | solution.py:180
  90.3 2.9 %collective-permute-done.8.b = bf16[64,3584]{1,0:T(8,128)(2,1)S(1)} collective-permute-done((bf16[64,3584]{1,0:T(8,128)(2,1)S(1)}, bf16[64,3584]{1,0:T(8,128)(2,1)S(1)}, u32[]{:S(2)}, u32[]{:S(2)}) %collective-permute-start.8) | collective-permute-done | bytes 458784 | tf_op jit(solution)/shard_map/ppermute | solution.py:180
  94.3 2.2 %collective-permute-start.9 = (bf16[256,3584]{1,0:T(8,128)(2,1)S(1)}, bf16[256,3584]{1,0:T(8,128)(2,1)S(1)}, u32[]{:S(2)}, u32[]{:S(2)}) collective-permute-start(bf16[256,3584]{1,0:T(8,128)(2,1)S(1)} %shard_map.92), channel_id=1, source_target_pairs={{0,1},{1,0},{2,3},{3,2},{4,5},{5,4},{6,7},{7,6},{8,9},{9,8},{10,11... | collective-permute-start | bytes 5505032 | tf_op jit(solution)/shard_map/ppermute | solution.py:180
  97.1 1.5 collective-permute-start.15
  101.3 2.7 %collective-permute-start.11 = (bf16[64,3584]{1,0:T(8,128)(2,1)S(1)}, bf16[64,3584]{1,0:T(8,128)(2,1)S(1)}, u32[]{:S(2)}, u32[]{:S(2)}) collective-permute-start(bf16[64,3584]{1,0:T(8,128)(2,1)S(1)} %get-tuple-element.50), channel_id=1, source_target_pairs={{0,2},{1,7},{2,4},{3,1},{4,6},{5,3},{6,0},{7,5},{8,10},{9,15},{10,... | collective-permute-start | bytes 1376264 | tf_op jit(solution)/shard_map/ppermute | solution.py:180
  104.5 10.4 %collective-permute-done.10.near = bf16[64,3584]{1,0:T(8,128)(2,1)S(1)} collective-permute-done((bf16[64,3584]{1,0:T(8,128)(2,1)S(1)}, bf16[64,3584]{1,0:T(8,128)(2,1)S(1)}, u32[]{:S(2)}, u32[]{:S(2)}) %collective-permute-start.10) | collective-permute-done | bytes 458784 | tf_op jit(solution)/shard_map/ppermute | solution.py:180
  114.9 8.9 %collective-permute-done.11.next_ = bf16[64,3584]{1,0:T(8,128)(2,1)S(1)} collective-permute-done((bf16[64,3584]{1,0:T(8,128)(2,1)S(1)}, bf16[64,3584]{1,0:T(8,128)(2,1)S(1)}, u32[]{:S(2)}, u32[]{:S(2)}) %collective-permute-start.11) | collective-permute-done | bytes 458784 | tf_op jit(solution)/shard_map/ppermute | solution.py:180
  124.3 6.2 %collective-permute-done.14.c = bf16[64,3584]{1,0:T(8,128)(2,1)S(1)} collective-permute-done((bf16[64,3584]{1,0:T(8,128)(2,1)S(1)}, bf16[64,3584]{1,0:T(8,128)(2,1)S(1)}, u32[]{:S(2)}, u32[]{:S(2)}) %collective-permute-start.14) | collective-permute-done | bytes 458784 | tf_op jit(solution)/shard_map/ppermute | solution.py:180
  130.4 1.8 %collective-permute-done.15.m_acts = bf16[3,512,256]{2,1,0:T(8,128)(2,1)S(1)} collective-permute-done((bf16[3,512,256]{2,1,0:T(8,128)(2,1)S(1)}, bf16[3,512,256]{2,1,0:T(8,128)(2,1)S(1)}, u32[]{:S(2)}, u32[]{:S(2)}) %collective-permute-start.15) | collective-permute-done | bytes 786464 | tf_op jit(solution)/shard_map/ppermute | solution.py:201
  132.8 4.9 %all-to-all-start.2 = ((bf16[8,8,3584]{2,1,0:T(8,128)(2,1)}), bf16[8,8,3584]{2,1,0:T(8,128)(2,1)}, u32[]{:S(2)}, u32[]{:S(2)}) async-start(bf16[8,8,3584]{2,1,0:T(8,128)(2,1)} %bitcast.8), calls=%async_computation.2 | async-start | bytes 917504 | tf_op jit(solution)/shard_map/all_to_all | solution.py:207
  137.7 1.5 copy-done.3
  139.2 1.5 copy-done.5
  140.7 1.5 copy-done.7
  142.2 7.9 %shard_map.96 = bf16[1,3,1792,256]{3,2,1,0:T(8,128)(2,1)} custom-call(s32[1]{0:T(128)} %bitcast.upper, bf16[256,3584]{1,0:T(8,128)(2,1)S(1)} %copy-done.3, bf16[256,3584]{1,0:T(8,128)(2,1)} %collective-permute-done.6.x_other.xo, bf16[256,3584]{1,0:T(8,128)(2,1)S(1)} %copy-done.5, bf16[256,3584]{1,0:T(8,128)(2,1)S(1)} %copy-done.7, ...), custom_call_target="tpu_custom_call" | custom-call | flops 100000000 | bytes 100000 | tf_op jit(solution)/shard_map/pallas_call | solution.py:158
  150.1 3.4 %all-to-all-done.2 = bf16[8,8,3584]{2,1,0:T(8,128)(2,1)} async-done(((bf16[8,8,3584]{2,1,0:T(8,128)(2,1)}), bf16[8,8,3584]{2,1,0:T(8,128)(2,1)}, u32[]{:S(2)}, u32[]{:S(2)}) %all-to-all-start.2) | async-done | bytes 458784 | tf_op jit(solution)/shard_map/all_to_all | solution.py:207
  153.5 2.3 %shard_map.97 = bf16[128,3584]{1,0:T(8,128)(2,1)} custom-call(bf16[128,64]{1,0:T(8,128)(2,1)S(1)} %get-tuple-element.32.select, bf16[64,3584]{1,0:T(8,128)(2,1)} %bitcast.6.rows), custom_call_target="tpu_custom_call" | custom-call | flops 1000000000 | bytes 1000000 | tf_op jit(solution)/shard_map/pallas_call | solution.py:31
  (53 shorter events, 18.3 us)
Async XLA Ops:
  2.2 1.2 copy-start.10
  3.4 1.2 copy-start.11
  33.9 9.0 %collective-permute-start.1 = (bf16[64,3584]{1,0:T(8,128)(2,1)S(1)}, bf16[64,3584]{1,0:T(8,128)(2,1)S(1)}, u32[]{:S(2)}, u32[]{:S(2)}) collective-permute-start(bf16[64,3584]{1,0:T(8,128)(2,1)S(1)} %bitcast.9), channel_id=1, source_target_pairs={{0,6},{1,3},{2,0},{3,5},{4,2},{5,7},{6,4},{7,1},{8,14},{9,11},{10,... | collective-permute-start | bytes 1376264 | tf_op jit(solution)/shard_map/ppermute | solution.py:180
  35.1 11.8 %collective-permute-start = (bf16[64,3584]{1,0:T(8,128)(2,1)S(1)}, bf16[64,3584]{1,0:T(8,128)(2,1)S(1)}, u32[]{:S(2)}, u32[]{:S(2)}) collective-permute-start(bf16[64,3584]{1,0:T(8,128)(2,1)S(1)} %bitcast.10), channel_id=1, source_target_pairs={{0,2},{1,7},{2,4},{3,1},{4,6},{5,3},{6,0},{7,5},{8,10},{9,15},{10,... | collective-permute-start | bytes 1376264 | tf_op jit(solution)/shard_map/ppermute | solution.py:180
  36.6 24.8 %all-to-all-start.1 = ((bf16[16,8,3584]{2,1,0:T(8,128)(2,1)}), bf16[16,8,3584]{2,1,0:T(8,128)(2,1)S(1)}, u32[]{:S(2)}, u32[]{:S(2)}) async-start(bf16[16,8,3584]{2,1,0:T(8,128)(2,1)} %bitcast.3), calls=%async_computation.1 | async-start | bytes 1835008 | tf_op jit(solution)/shard_map/all_to_all | solution.py:223
  47.0 7.6 %collective-permute-start.2 = (bf16[64,3584]{1,0:T(8,128)(2,1)S(1)}, bf16[64,3584]{1,0:T(8,128)(2,1)S(1)}, u32[]{:S(2)}, u32[]{:S(2)}) collective-permute-start(bf16[64,3584]{1,0:T(8,128)(2,1)S(1)} %collective-permute-done.b), channel_id=1, source_target_pairs={{0,2},{1,7},{2,4},{3,1},{4,6},{5,3},{6,0},{7,5},{8,10},{9,15},{10,... | collective-permute-start | bytes 1376264 | tf_op jit(solution)/shard_map/ppermute | solution.py:180
  54.6 1.0 copy-start.13
  56.7 20.2 %copy-start.2 = (bf16[256,3584]{1,0:T(8,128)(2,1)}, bf16[256,3584]{1,0:T(8,128)(2,1)S(1)}, u32[]{:S(2)}) copy-start(bf16[256,3584]{1,0:T(8,128)(2,1)S(1)} %shard_map.88.x_mine.xm) | copy-start | bytes 5505028
  56.7 20.2 %collective-permute-start.6 = (bf16[256,3584]{1,0:T(8,128)(2,1)S(1)}, bf16[256,3584]{1,0:T(8,128)(2,1)}, u32[]{:S(2)}, u32[]{:S(2)}) collective-permute-start(bf16[256,3584]{1,0:T(8,128)(2,1)S(1)} %shard_map.88.x_mine.xm), channel_id=1, source_target_pairs={{0,1},{1,0},{2,3},{3,2},{4,5},{5,4},{6,7},{7,6},{8,9},{9,8},{10,11... | collective-permute-start | bytes 5505032 | tf_op jit(solution)/shard_map/ppermute | solution.py:180
  61.4 15.6 %copy-start = (bf16[1,3584,256]{2,1,0:T(8,128)(2,1)S(1)}, bf16[1,3584,256]{2,1,0:T(8,128)(2,1)}, u32[]{:S(2)}) copy-start(bf16[1,3584,256]{2,1,0:T(8,128)(2,1)} %w_gate.5) | copy-start | bytes 5505028
  61.4 15.6 %copy-start.1 = (bf16[1,3584,256]{2,1,0:T(8,128)(2,1)S(1)}, bf16[1,3584,256]{2,1,0:T(8,128)(2,1)}, u32[]{:S(2)}) copy-start(bf16[1,3584,256]{2,1,0:T(8,128)(2,1)} %w_up.5) | copy-start | bytes 5505028
  61.4 9.8 %collective-permute-start.4 = (bf16[64,3584]{1,0:T(8,128)(2,1)S(1)}, bf16[64,3584]{1,0:T(8,128)(2,1)S(1)}, u32[]{:S(2)}, u32[]{:S(2)}) collective-permute-start(bf16[64,3584]{1,0:T(8,128)(2,1)S(1)} %get-tuple-element.39.a), channel_id=1, source_target_pairs={{0,6},{1,3},{2,0},{3,5},{4,2},{5,7},{6,4},{7,1},{8,14},{9,11},{10,... | collective-permute-start | bytes 1376264 | tf_op jit(solution)/shard_map/ppermute | solution.py:180
  61.5 12.0 %collective-permute-start.3 = (bf16[64,3584]{1,0:T(8,128)(2,1)S(1)}, bf16[64,3584]{1,0:T(8,128)(2,1)S(1)}, u32[]{:S(2)}, u32[]{:S(2)}) collective-permute-start(bf16[64,3584]{1,0:T(8,128)(2,1)S(1)} %get-tuple-element.39.a), channel_id=1, source_target_pairs={{0,2},{1,7},{2,4},{3,1},{4,6},{5,3},{6,0},{7,5},{8,10},{9,15},{10,... | collective-permute-start | bytes 1376264 | tf_op jit(solution)/shard_map/ppermute | solution.py:180
  73.5 8.8 %collective-permute-start.5 = (bf16[64,3584]{1,0:T(8,128)(2,1)S(1)}, bf16[64,3584]{1,0:T(8,128)(2,1)S(1)}, u32[]{:S(2)}, u32[]{:S(2)}) collective-permute-start(bf16[64,3584]{1,0:T(8,128)(2,1)S(1)} %collective-permute-done.3.b), channel_id=1, source_target_pairs={{0,2},{1,7},{2,4},{3,1},{4,6},{5,3},{6,0},{7,5},{8,10},{9,15},{10,... | collective-permute-start | bytes 1376264 | tf_op jit(solution)/shard_map/ppermute | solution.py:180
  82.4 6.6 %copy-start.9 = (bf16[1,256,3584]{2,1,0:T(8,128)(2,1)S(1)}, bf16[1,256,3584]{2,1,0:T(8,128)(2,1)}, u32[]{:S(2)}) copy-start(bf16[1,256,3584]{2,1,0:T(8,128)(2,1)} %w_down.1) | copy-start | bytes 5505028
  82.5 7.8 %copy-start.4 = (bf16[256,3584]{1,0:T(8,128)(2,1)}, bf16[256,3584]{1,0:T(8,128)(2,1)S(1)}, u32[]{:S(2)}) copy-start(bf16[256,3584]{1,0:T(8,128)(2,1)S(1)} %shard_map.90.g_mine.gm) | copy-start | bytes 5505028
  82.5 6.5 %collective-permute-start.7 = (bf16[256,3584]{1,0:T(8,128)(2,1)S(1)}, bf16[256,3584]{1,0:T(8,128)(2,1)S(1)}, u32[]{:S(2)}, u32[]{:S(2)}) collective-permute-start(bf16[256,3584]{1,0:T(8,128)(2,1)S(1)} %shard_map.90.g_mine.gm), channel_id=1, source_target_pairs={{0,1},{1,0},{2,3},{3,2},{4,5},{5,4},{6,7},{7,6},{8,9},{9,8},{10,11... | collective-permute-start | bytes 5505032 | tf_op jit(solution)/shard_map/ppermute | solution.py:180
  85.6 7.6 %collective-permute-start.8 = (bf16[64,3584]{1,0:T(8,128)(2,1)S(1)}, bf16[64,3584]{1,0:T(8,128)(2,1)S(1)}, u32[]{:S(2)}, u32[]{:S(2)}) collective-permute-start(bf16[64,3584]{1,0:T(8,128)(2,1)S(1)} %get-tuple-element.46.a), channel_id=1, source_target_pairs={{0,2},{1,7},{2,4},{3,1},{4,6},{5,3},{6,0},{7,5},{8,10},{9,15},{10,... | collective-permute-start | bytes 1376264 | tf_op jit(solution)/shard_map/ppermute | solution.py:180
  89.0 1.3 copy-start.6
  94.3 5.7 %collective-permute-start.9 = (bf16[256,3584]{1,0:T(8,128)(2,1)S(1)}, bf16[256,3584]{1,0:T(8,128)(2,1)S(1)}, u32[]{:S(2)}, u32[]{:S(2)}) collective-permute-start(bf16[256,3584]{1,0:T(8,128)(2,1)S(1)} %shard_map.92), channel_id=1, source_target_pairs={{0,1},{1,0},{2,3},{3,2},{4,5},{5,4},{6,7},{7,6},{8,9},{9,8},{10,11... | collective-permute-start | bytes 5505032 | tf_op jit(solution)/shard_map/ppermute | solution.py:180
  96.6 7.6 %collective-permute-start.13 = (bf16[64,3584]{1,0:T(8,128)(2,1)S(1)}, bf16[64,3584]{1,0:T(8,128)(2,1)S(1)}, u32[]{:S(2)}, u32[]{:S(2)}) collective-permute-start(bf16[64,3584]{1,0:T(8,128)(2,1)S(1)} %collective-permute-done.8.b), channel_id=1, source_target_pairs={{0,2},{1,7},{2,4},{3,1},{4,6},{5,3},{6,0},{7,5},{8,10},{9,15},{10,... | collective-permute-start | bytes 1376264 | tf_op jit(solution)/shard_map/ppermute | solution.py:180
  97.1 35.1 %collective-permute-start.15 = (bf16[3,512,256]{2,1,0:T(8,128)(2,1)S(1)}, bf16[3,512,256]{2,1,0:T(8,128)(2,1)S(1)}, u32[]{:S(2)}, u32[]{:S(2)}) collective-permute-start(bf16[3,512,256]{2,1,0:T(8,128)(2,1)S(1)} %shard_map.91.acts), channel_id=1, source_target_pairs={{0,192},{64,128},{128,64},{192,0},{1,193},{65,129},{129,65},{193,1... | collective-permute-start | bytes 2359304 | tf_op jit(solution)/shard_map/ppermute | solution.py:201
  101.2 13.8 %collective-permute-start.10 = (bf16[64,3584]{1,0:T(8,128)(2,1)S(1)}, bf16[64,3584]{1,0:T(8,128)(2,1)S(1)}, u32[]{:S(2)}, u32[]{:S(2)}) collective-permute-start(bf16[64,3584]{1,0:T(8,128)(2,1)S(1)} %get-tuple-element.49), channel_id=1, source_target_pairs={{0,6},{1,3},{2,0},{3,5},{4,2},{5,7},{6,4},{7,1},{8,14},{9,11},{10,... | collective-permute-start | bytes 1376264 | tf_op jit(solution)/shard_map/ppermute | solution.py:180
  101.3 22.6 %collective-permute-start.11 = (bf16[64,3584]{1,0:T(8,128)(2,1)S(1)}, bf16[64,3584]{1,0:T(8,128)(2,1)S(1)}, u32[]{:S(2)}, u32[]{:S(2)}) collective-permute-start(bf16[64,3584]{1,0:T(8,128)(2,1)S(1)} %get-tuple-element.50), channel_id=1, source_target_pairs={{0,2},{1,7},{2,4},{3,1},{4,6},{5,3},{6,0},{7,5},{8,10},{9,15},{10,... | collective-permute-start | bytes 1376264 | tf_op jit(solution)/shard_map/ppermute | solution.py:180
  103.9 20.1 %collective-permute-start.12 = (bf16[64,3584]{1,0:T(8,128)(2,1)S(1)}, bf16[64,3584]{1,0:T(8,128)(2,1)S(1)}, u32[]{:S(2)}, u32[]{:S(2)}) collective-permute-start(bf16[64,3584]{1,0:T(8,128)(2,1)S(1)} %get-tuple-element.51), channel_id=1, source_target_pairs={{0,4},{1,5},{2,6},{3,7},{4,0},{5,1},{6,2},{7,3},{8,12},{9,13},{10,... | collective-permute-start | bytes 1376264 | tf_op jit(solution)/shard_map/ppermute | solution.py:180
  104.2 26.2 %collective-permute-start.14 = (bf16[64,3584]{1,0:T(8,128)(2,1)S(1)}, bf16[64,3584]{1,0:T(8,128)(2,1)S(1)}, u32[]{:S(2)}, u32[]{:S(2)}) collective-permute-start(bf16[64,3584]{1,0:T(8,128)(2,1)S(1)} %get-tuple-element.46.a), channel_id=1, source_target_pairs={{0,6},{1,3},{2,0},{3,5},{4,2},{5,7},{6,4},{7,1},{8,14},{9,11},{10,... | collective-permute-start | bytes 1376264 | tf_op jit(solution)/shard_map/ppermute | solution.py:180
  124.2 8.1 %copy-start.8 = (bf16[64,3584]{1,0:T(8,128)(2,1)}, bf16[64,3584]{1,0:T(8,128)(2,1)S(1)}, u32[]{:S(2)}) copy-start(bf16[64,3584]{1,0:T(8,128)(2,1)S(1)} %shard_map.94) | copy-start | bytes 1376260
  132.3 5.4 %collective-permute-start.16 = (bf16[256,3584]{1,0:T(8,128)(2,1)S(1)}, bf16[256,3584]{1,0:T(8,128)(2,1)}, u32[]{:S(2)}, u32[]{:S(2)}) collective-permute-start(bf16[256,3584]{1,0:T(8,128)(2,1)S(1)} %shard_map.95.mxm.mgm), channel_id=1, source_target_pairs={{0,1},{1,0},{2,3},{3,2},{4,5},{5,4},{6,7},{7,6},{8,9},{9,8},{10,11... | collective-permute-start | bytes 5505032 | tf_op jit(solution)/shard_map/ppermute | solution.py:180
  132.8 20.7 %all-to-all-start.2 = ((bf16[8,8,3584]{2,1,0:T(8,128)(2,1)}), bf16[8,8,3584]{2,1,0:T(8,128)(2,1)}, u32[]{:S(2)}, u32[]{:S(2)}) async-start(bf16[8,8,3584]{2,1,0:T(8,128)(2,1)} %bitcast.8), calls=%async_computation.2 | async-start | bytes 917504 | tf_op jit(solution)/shard_map/all_to_all | solution.py:207
  137.7 1.5 copy-start.3
  139.2 1.5 copy-start.5
  140.7 1.5 copy-start.7
  (3 other events, 2.6 us)

commit v4 on v3

--- a/solution.py
+++ b/solution.py
@@ -285,7 +285,7 @@
     total = run(total_kernel, [rows], own, near, next_, far)[0]
     m_far, m_next, m_acts, _ = together(m_far, m_next, m_acts, total)
     m_mine = pack(m_here, m_near, m_next, m_far, us=10.0)
-    m_other = other_core(m_mine)
+    m_other = pack(*(other_core(piece) for piece in (m_here, m_near, m_next, m_far)))
     returned = across_groups(total)
     weight_grads = weight_grads_of(
         upper, x_mine, x_other, g_mine, g_other, m_mine, m_other, acts, m_acts

time: 157 us -> 156 us (level)
  waiting for transfers between devices: 60.4 us -> 54.6 us
  starting transfers between devices: 35.3 us -> 39.1 us
  Pallas kernels: 19.8 us -> 22.8 us
  local copies, waits for them, and re-layouts: 12 us -> 10.2 us
    ppermute x16 -> x19, waiting for transfers between devices: 54.7 us -> 50.8 us  [permute_members(): return lax.ppermute(value, 'expert', pairs)]
    pallas_call x11 -> x12, Pallas kernels: 12 us -> 15.4 us  [run(): pl.pallas_call(kernel, out_shape=[jax.ShapeDtypeStruct(shape, dtype) for...]
    ppermute x16 -> x19, starting transfers between devices: 25.3 us -> 27.9 us  [permute_members(): return lax.ppermute(value, 'expert', pairs)]
    unnamed x34, local copies, waits for them, and re-layouts: 12 us -> 10.2 us
    ppermute x1, waiting for transfers between devices: 1.77 us -> 0.01 us  [mirror(): lax.ppermute(value, 'pipe', [(k, count - 1 - k) for k in range(count)])]
  transfers between devices with their start and end apart: 19 -> 22, of which waited for: 17 -> 12; matrix products, arithmetic and copies ran while one was open for 0% -> 0% of each run, Pallas kernels for 9% -> 11%
where the time goes in v4:
time: 156 us; the launch traced here: 155 us
  waiting for transfers between devices  54.6 us (35%)
  starting transfers between devices  39.1 us (25%)
  blocking collectives  27.4 us (18%)
  Pallas kernels  22.8 us (15%)
  local copies, waits for them, and re-layouts  10.2 us (7%)
    ppermute x19, waiting for transfers between devices, permute_members(): return lax.ppermute(value, 'expert', pairs)  50.8 us
    ppermute x19, starting transfers between devices, permute_members(): return lax.ppermute(value, 'expert', pairs)  27.9 us
    all_to_all x1, blocking collectives, across_groups(): lax.all_to_all(value, 'expert', split_axis=0, concat_axis=0, axis_index_g...  27.4 us
    pallas_call x12, Pallas kernels, run(): pl.pallas_call(kernel, out_shape=[jax.ShapeDtypeStruct(shape, dtype) for...  15.4 us
    unnamed x34, local copies, waits for them, and re-layouts  10.2 us
    pallas_call x1, Pallas kernels, weight_grads_of(): pl.pallas_call(weights_kernel, out_shape=jax.ShapeDtypeStruct((1, 3, feat...  7.35 us
    all_to_all x1, starting transfers between devices, across_groups(): lax.all_to_all(value, 'expert', split_axis=0, concat_axis=0, axis_index_g...  5.72 us
    all_to_all x1, waiting for transfers between devices, across_groups(): lax.all_to_all(value, 'expert', split_axis=0, concat_axis=0, axis_index_g...  3.79 us
  transfers between devices with their start and end apart: 22, of which 12 were waited for; matrix products, arithmetic and copies ran while one was open for 0% of the time, Pallas kernels for 11%

profile of v4, /device:TPU:33, one launch (start us, length us, event | category | flops | bytes accessed | tf_op | source)
XLA Modules:
  0.0 155.0 jit_solution(11825956776365325044)
XLA Ops:
  2.2 1.2 copy-done.8
  3.4 1.2 copy-done.9
  4.6 1.9 %shard_map.86 = (bf16[64,3584]{1,0:T(8,128)(2,1)S(1)}, bf16[128,3584]{1,0:T(8,128)(2,1)}, bf16[128,64]{1,0:T(8,128)(2,1)S(1)}) custom-call(s32[1]{0:T(128)} %bitcast.upper, bf16[128,3584]{1,0:T(8,128)(2,1)S(1)} %copy-done.8, bf16[128,3584]{1,0:T(8,128)(2,1)S(1)} %copy-done.9, bf16[128,8]{1,0:T(8,128)(2,1)S(1)} %copy.9.probs, s32[128,8]{1,0:T(8,128)S(1)} %copy.10.ids), custom_call_target="tpu_custom_call" | custom-call | flops 1000000000 | bytes 1000000 | tf_op jit(solution)/shard_map/pallas_call | solution.py:31
  6.5 27.4 %all_to_all.35 = bf16[8,8,3584]{2,1,0:T(8,128)(2,1)S(1)} all-to-all(bf16[8,8,3584]{2,1,0:T(8,128)(2,1)S(1)} %bitcast.12), channel_id=1, replica_groups={{0,8,16,24,32,40,48,56},{1,9,17,25,33,41,49,57},{2,10,18,26,34,42,50,58..., dimensions={0} | all-to-all | bytes 917504 | tf_op jit(solution)/shard_map/all_to_all | solution.py:207
  33.9 2.5 %collective-permute-start = (bf16[64,3584]{1,0:T(8,128)(2,1)S(1)}, bf16[64,3584]{1,0:T(8,128)(2,1)S(1)}, u32[]{:S(2)}, u32[]{:S(2)}) collective-permute-start(bf16[64,3584]{1,0:T(8,128)(2,1)S(1)} %bitcast.9), channel_id=1, source_target_pairs={{0,2},{1,7},{2,4},{3,1},{4,6},{5,3},{6,0},{7,5},{8,10},{9,15},{10,... | collective-permute-start | bytes 1376264 | tf_op jit(solution)/shard_map/ppermute | solution.py:180
  36.4 3.6 %all-to-all-start.1 = ((bf16[16,8,3584]{2,1,0:T(8,128)(2,1)}), bf16[16,8,3584]{2,1,0:T(8,128)(2,1)S(1)}, u32[]{:S(2)}, u32[]{:S(2)}) async-start(bf16[16,8,3584]{2,1,0:T(8,128)(2,1)} %bitcast.3), calls=%async_computation.1 | async-start | bytes 1835008 | tf_op jit(solution)/shard_map/all_to_all | solution.py:223
  40.0 4.2 %collective-permute-done.b = bf16[64,3584]{1,0:T(8,128)(2,1)S(1)} collective-permute-done((bf16[64,3584]{1,0:T(8,128)(2,1)S(1)}, bf16[64,3584]{1,0:T(8,128)(2,1)S(1)}, u32[]{:S(2)}, u32[]{:S(2)}) %collective-permute-start) | collective-permute-done | bytes 458784 | tf_op jit(solution)/shard_map/ppermute | solution.py:180
  44.2 5.1 %collective-permute-done.1.c = bf16[64,3584]{1,0:T(8,128)(2,1)S(1)} collective-permute-done((bf16[64,3584]{1,0:T(8,128)(2,1)S(1)}, bf16[64,3584]{1,0:T(8,128)(2,1)S(1)}, u32[]{:S(2)}, u32[]{:S(2)}) %collective-permute-start.1) | collective-permute-done | bytes 458784 | tf_op jit(solution)/shard_map/ppermute | solution.py:180
  50.9 6.9 %collective-permute-done.2.d = bf16[64,3584]{1,0:T(8,128)(2,1)S(1)} collective-permute-done((bf16[64,3584]{1,0:T(8,128)(2,1)S(1)}, bf16[64,3584]{1,0:T(8,128)(2,1)S(1)}, u32[]{:S(2)}, u32[]{:S(2)}) %collective-permute-start.2) | collective-permute-done | bytes 458784 | tf_op jit(solution)/shard_map/ppermute | solution.py:180
  59.9 2.4 %collective-permute-start.6 = (bf16[256,3584]{1,0:T(8,128)(2,1)S(1)}, bf16[256,3584]{1,0:T(8,128)(2,1)}, u32[]{:S(2)}, u32[]{:S(2)}) collective-permute-start(bf16[256,3584]{1,0:T(8,128)(2,1)S(1)} %shard_map.88.x_mine.xm), channel_id=1, source_target_pairs={{0,1},{1,0},{2,3},{3,2},{4,5},{5,4},{6,7},{7,6},{8,9},{9,8},{10,11... | collective-permute-start | bytes 5505032 | tf_op jit(solution)/shard_map/ppermute | solution.py:180
  63.1 1.7 %collective-permute-start.3 = (bf16[64,3584]{1,0:T(8,128)(2,1)S(1)}, bf16[64,3584]{1,0:T(8,128)(2,1)S(1)}, u32[]{:S(2)}, u32[]{:S(2)}) collective-permute-start(bf16[64,3584]{1,0:T(8,128)(2,1)S(1)} %get-tuple-element.39.a), channel_id=1, source_target_pairs={{0,2},{1,7},{2,4},{3,1},{4,6},{5,3},{6,0},{7,5},{8,10},{9,15},{10,... | collective-permute-start | bytes 1376264 | tf_op jit(solution)/shard_map/ppermute | solution.py:180
  64.8 10.3 %collective-permute-done.3.b = bf16[64,3584]{1,0:T(8,128)(2,1)S(1)} collective-permute-done((bf16[64,3584]{1,0:T(8,128)(2,1)S(1)}, bf16[64,3584]{1,0:T(8,128)(2,1)S(1)}, u32[]{:S(2)}, u32[]{:S(2)}) %collective-permute-start.3) | collective-permute-done | bytes 458784 | tf_op jit(solution)/shard_map/ppermute | solution.py:180
  75.0 2.0 %collective-permute-done.4.c = bf16[64,3584]{1,0:T(8,128)(2,1)S(1)} collective-permute-done((bf16[64,3584]{1,0:T(8,128)(2,1)S(1)}, bf16[64,3584]{1,0:T(8,128)(2,1)S(1)}, u32[]{:S(2)}, u32[]{:S(2)}) %collective-permute-start.4) | collective-permute-done | bytes 458784 | tf_op jit(solution)/shard_map/ppermute | solution.py:180
  77.1 3.5 %shard_map.89 = (f32[512,256]{1,0:T(8,128)S(1)}, f32[512,256]{1,0:T(8,128)S(1)}) custom-call(bf16[256,3584]{1,0:T(8,128)(2,1)S(1)} %shard_map.88.x_mine.xm, bf16[256,3584]{1,0:T(8,128)(2,1)} %collective-permute-done.6.x_other.xo, bf16[1,3584,256]{2,1,0:T(8,128)(2,1)S(1)} %copy-done, bf16[1,3584,256]{2,1,0:T(8,128)(2,1)S(1)} %copy-done.1), custom_call_target="tpu_custom_call" | custom-call | flops 3000000000 | bytes 3000000 | tf_op jit(solution)/shard_map/pallas_call | solution.py:31
  80.6 4.0 %collective-permute-done.5.d = bf16[64,3584]{1,0:T(8,128)(2,1)S(1)} collective-permute-done((bf16[64,3584]{1,0:T(8,128)(2,1)S(1)}, bf16[64,3584]{1,0:T(8,128)(2,1)S(1)}, u32[]{:S(2)}, u32[]{:S(2)}) %collective-permute-start.5) | collective-permute-done | bytes 458784 | tf_op jit(solution)/shard_map/ppermute | solution.py:180
  84.8 1.7 %collective-permute-start.7 = (bf16[256,3584]{1,0:T(8,128)(2,1)S(1)}, bf16[256,3584]{1,0:T(8,128)(2,1)S(1)}, u32[]{:S(2)}, u32[]{:S(2)}) collective-permute-start(bf16[256,3584]{1,0:T(8,128)(2,1)S(1)} %shard_map.90.g_mine.gm), channel_id=1, source_target_pairs={{0,1},{1,0},{2,3},{3,2},{4,5},{5,4},{6,7},{7,6},{8,9},{9,8},{10,11... | collective-permute-start | bytes 5505032 | tf_op jit(solution)/shard_map/ppermute | solution.py:180
  87.6 2.3 %collective-permute-done.7.g_other.go = bf16[256,3584]{1,0:T(8,128)(2,1)S(1)} collective-permute-done((bf16[256,3584]{1,0:T(8,128)(2,1)S(1)}, bf16[256,3584]{1,0:T(8,128)(2,1)S(1)}, u32[]{:S(2)}, u32[]{:S(2)}) %collective-permute-start.7) | collective-permute-done | bytes 1835040 | tf_op jit(solution)/shard_map/ppermute | solution.py:180
  89.9 1.3 shard_map.91.acts
  91.2 3.2 %collective-permute-done.8.b = bf16[64,3584]{1,0:T(8,128)(2,1)} collective-permute-done((bf16[64,3584]{1,0:T(8,128)(2,1)}, bf16[64,3584]{1,0:T(8,128)(2,1)}, u32[]{:S(2)}, u32[]{:S(2)}) %collective-permute-start.8) | collective-permute-done | bytes 458784 | tf_op jit(solution)/shard_map/ppermute | solution.py:180
  95.6 2.2 %collective-permute-start.9 = (bf16[256,3584]{1,0:T(8,128)(2,1)S(1)}, bf16[256,3584]{1,0:T(8,128)(2,1)S(1)}, u32[]{:S(2)}, u32[]{:S(2)}) collective-permute-start(bf16[256,3584]{1,0:T(8,128)(2,1)S(1)} %shard_map.92), channel_id=1, source_target_pairs={{0,1},{1,0},{2,3},{3,2},{4,5},{5,4},{6,7},{7,6},{8,9},{9,8},{10,11... | collective-permute-start | bytes 5505032 | tf_op jit(solution)/shard_map/ppermute | solution.py:180
  98.0 1.9 %collective-permute-start.15 = (bf16[3,512,256]{2,1,0:T(8,128)(2,1)S(1)}, bf16[3,512,256]{2,1,0:T(8,128)(2,1)S(1)}, u32[]{:S(2)}, u32[]{:S(2)}) collective-permute-start(bf16[3,512,256]{2,1,0:T(8,128)(2,1)S(1)} %shard_map.91.acts), channel_id=1, source_target_pairs={{0,192},{64,128},{128,64},{192,0},{1,193},{65,129},{129,65},{193,1... | collective-permute-start | bytes 2359304 | tf_op jit(solution)/shard_map/ppermute | solution.py:201
  99.9 1.3 collective-permute-done.9.arrived
  102.6 2.5 %collective-permute-start.11 = (bf16[64,3584]{1,0:T(8,128)(2,1)S(1)}, bf16[64,3584]{1,0:T(8,128)(2,1)S(1)}, u32[]{:S(2)}, u32[]{:S(2)}) collective-permute-start(bf16[64,3584]{1,0:T(8,128)(2,1)S(1)} %get-tuple-element.50), channel_id=1, source_target_pairs={{0,2},{1,7},{2,4},{3,1},{4,6},{5,3},{6,0},{7,5},{8,10},{9,15},{10,... | collective-permute-start | bytes 1376264 | tf_op jit(solution)/shard_map/ppermute | solution.py:180
  105.7 11.0 %collective-permute-done.10.near = bf16[64,3584]{1,0:T(8,128)(2,1)S(1)} collective-permute-done((bf16[64,3584]{1,0:T(8,128)(2,1)S(1)}, bf16[64,3584]{1,0:T(8,128)(2,1)S(1)}, u32[]{:S(2)}, u32[]{:S(2)}) %collective-permute-start.10) | collective-permute-done | bytes 458784 | tf_op jit(solution)/shard_map/ppermute | solution.py:180
  116.7 8.8 %collective-permute-start.16 = (bf16[64,3584]{1,0:T(8,128)(2,1)}, bf16[64,3584]{1,0:T(8,128)(2,1)}, u32[]{:S(2)}, u32[]{:S(2)}) collective-permute-start(bf16[64,3584]{1,0:T(8,128)(2,1)} %get-tuple-element.46.a), channel_id=1, source_target_pairs={{0,1},{1,0},{2,3},{3,2},{4,5},{5,4},{6,7},{7,6},{8,9},{9,8},{10,11... | collective-permute-start | bytes 1376264 | tf_op jit(solution)/shard_map/ppermute | solution.py:180
  125.5 3.9 %collective-permute-start.17 = (bf16[64,3584]{1,0:T(8,128)(2,1)}, bf16[64,3584]{1,0:T(8,128)(2,1)}, u32[]{:S(2)}, u32[]{:S(2)}) collective-permute-start(bf16[64,3584]{1,0:T(8,128)(2,1)} %collective-permute-done.8.b), channel_id=1, source_target_pairs={{0,1},{1,0},{2,3},{3,2},{4,5},{5,4},{6,7},{7,6},{8,9},{9,8},{10,11... | collective-permute-start | bytes 1376264 | tf_op jit(solution)/shard_map/ppermute | solution.py:180
  130.4 5.7 %all-to-all-start.2 = ((bf16[8,8,3584]{2,1,0:T(8,128)(2,1)}), bf16[8,8,3584]{2,1,0:T(8,128)(2,1)}, u32[]{:S(2)}, u32[]{:S(2)}) async-start(bf16[8,8,3584]{2,1,0:T(8,128)(2,1)} %bitcast.8), calls=%async_computation.2 | async-start | bytes 917504 | tf_op jit(solution)/shard_map/all_to_all | solution.py:207
  137.8 1.4 shard_map.95.mxm.mgm
  139.3 1.4 shard_map.96.mxo.mgo
  141.5 7.4 %shard_map.97 = bf16[1,3,1792,256]{3,2,1,0:T(8,128)(2,1)} custom-call(s32[1]{0:T(128)} %bitcast.upper, bf16[256,3584]{1,0:T(8,128)(2,1)S(1)} %shard_map.88.x_mine.xm, bf16[256,3584]{1,0:T(8,128)(2,1)} %collective-permute-done.6.x_other.xo, bf16[256,3584]{1,0:T(8,128)(2,1)S(1)} %copy-done.3, bf16[256,3584]{1,0:T(8,128)(2,1)S(1)} %copy-done.5, ...), custom_call_target="tpu_custom_call" | custom-call | flops 100000000 | bytes 100000 | tf_op jit(solution)/shard_map/pallas_call | solution.py:158
  148.9 3.8 %all-to-all-done.2 = bf16[8,8,3584]{2,1,0:T(8,128)(2,1)} async-done(((bf16[8,8,3584]{2,1,0:T(8,128)(2,1)}), bf16[8,8,3584]{2,1,0:T(8,128)(2,1)}, u32[]{:S(2)}, u32[]{:S(2)}) %all-to-all-start.2) | async-done | bytes 458784 | tf_op jit(solution)/shard_map/all_to_all | solution.py:207
  152.7 2.3 %shard_map.98 = bf16[128,3584]{1,0:T(8,128)(2,1)} custom-call(bf16[128,64]{1,0:T(8,128)(2,1)S(1)} %get-tuple-element.32.select, bf16[64,3584]{1,0:T(8,128)(2,1)} %bitcast.6.rows), custom_call_target="tpu_custom_call" | custom-call | flops 1000000000 | bytes 1000000 | tf_op jit(solution)/shard_map/pallas_call | solution.py:31
  (60 shorter events, 14.1 us)
Async XLA Ops:
  2.2 1.2 copy-start.8
  3.4 1.2 copy-start.9
  33.9 10.3 %collective-permute-start = (bf16[64,3584]{1,0:T(8,128)(2,1)S(1)}, bf16[64,3584]{1,0:T(8,128)(2,1)S(1)}, u32[]{:S(2)}, u32[]{:S(2)}) collective-permute-start(bf16[64,3584]{1,0:T(8,128)(2,1)S(1)} %bitcast.9), channel_id=1, source_target_pairs={{0,2},{1,7},{2,4},{3,1},{4,6},{5,3},{6,0},{7,5},{8,10},{9,15},{10,... | collective-permute-start | bytes 1376264 | tf_op jit(solution)/shard_map/ppermute | solution.py:180
  36.4 12.9 %collective-permute-start.1 = (bf16[64,3584]{1,0:T(8,128)(2,1)S(1)}, bf16[64,3584]{1,0:T(8,128)(2,1)S(1)}, u32[]{:S(2)}, u32[]{:S(2)}) collective-permute-start(bf16[64,3584]{1,0:T(8,128)(2,1)S(1)} %bitcast.10), channel_id=1, source_target_pairs={{0,6},{1,3},{2,0},{3,5},{4,2},{5,7},{6,4},{7,1},{8,14},{9,11},{10,... | collective-permute-start | bytes 1376264 | tf_op jit(solution)/shard_map/ppermute | solution.py:180
  36.4 25.9 %all-to-all-start.1 = ((bf16[16,8,3584]{2,1,0:T(8,128)(2,1)}), bf16[16,8,3584]{2,1,0:T(8,128)(2,1)S(1)}, u32[]{:S(2)}, u32[]{:S(2)}) async-start(bf16[16,8,3584]{2,1,0:T(8,128)(2,1)} %bitcast.3), calls=%async_computation.1 | async-start | bytes 1835008 | tf_op jit(solution)/shard_map/all_to_all | solution.py:223
  50.1 7.6 %collective-permute-start.2 = (bf16[64,3584]{1,0:T(8,128)(2,1)S(1)}, bf16[64,3584]{1,0:T(8,128)(2,1)S(1)}, u32[]{:S(2)}, u32[]{:S(2)}) collective-permute-start(bf16[64,3584]{1,0:T(8,128)(2,1)S(1)} %collective-permute-done.b), channel_id=1, source_target_pairs={{0,2},{1,7},{2,4},{3,1},{4,6},{5,3},{6,0},{7,5},{8,10},{9,15},{10,... | collective-permute-start | bytes 1376264 | tf_op jit(solution)/shard_map/ppermute | solution.py:180
  59.9 17.2 %collective-permute-start.6 = (bf16[256,3584]{1,0:T(8,128)(2,1)S(1)}, bf16[256,3584]{1,0:T(8,128)(2,1)}, u32[]{:S(2)}, u32[]{:S(2)}) collective-permute-start(bf16[256,3584]{1,0:T(8,128)(2,1)S(1)} %shard_map.88.x_mine.xm), channel_id=1, source_target_pairs={{0,1},{1,0},{2,3},{3,2},{4,5},{5,4},{6,7},{7,6},{8,9},{9,8},{10,11... | collective-permute-start | bytes 5505032 | tf_op jit(solution)/shard_map/ppermute | solution.py:180
  62.3 14.8 %copy-start = (bf16[1,3584,256]{2,1,0:T(8,128)(2,1)S(1)}, bf16[1,3584,256]{2,1,0:T(8,128)(2,1)}, u32[]{:S(2)}) copy-start(bf16[1,3584,256]{2,1,0:T(8,128)(2,1)} %w_gate.5) | copy-start | bytes 5505028
  62.3 14.8 %copy-start.1 = (bf16[1,3584,256]{2,1,0:T(8,128)(2,1)S(1)}, bf16[1,3584,256]{2,1,0:T(8,128)(2,1)}, u32[]{:S(2)}) copy-start(bf16[1,3584,256]{2,1,0:T(8,128)(2,1)} %w_up.5) | copy-start | bytes 5505028
  63.1 11.9 %collective-permute-start.3 = (bf16[64,3584]{1,0:T(8,128)(2,1)S(1)}, bf16[64,3584]{1,0:T(8,128)(2,1)S(1)}, u32[]{:S(2)}, u32[]{:S(2)}) collective-permute-start(bf16[64,3584]{1,0:T(8,128)(2,1)S(1)} %get-tuple-element.39.a), channel_id=1, source_target_pairs={{0,2},{1,7},{2,4},{3,1},{4,6},{5,3},{6,0},{7,5},{8,10},{9,15},{10,... | collective-permute-start | bytes 1376264 | tf_op jit(solution)/shard_map/ppermute | solution.py:180
  64.8 12.3 %collective-permute-start.4 = (bf16[64,3584]{1,0:T(8,128)(2,1)S(1)}, bf16[64,3584]{1,0:T(8,128)(2,1)S(1)}, u32[]{:S(2)}, u32[]{:S(2)}) collective-permute-start(bf16[64,3584]{1,0:T(8,128)(2,1)S(1)} %get-tuple-element.39.a), channel_id=1, source_target_pairs={{0,6},{1,3},{2,0},{3,5},{4,2},{5,7},{6,4},{7,1},{8,14},{9,11},{10,... | collective-permute-start | bytes 1376264 | tf_op jit(solution)/shard_map/ppermute | solution.py:180
  77.0 7.6 %collective-permute-start.5 = (bf16[64,3584]{1,0:T(8,128)(2,1)S(1)}, bf16[64,3584]{1,0:T(8,128)(2,1)S(1)}, u32[]{:S(2)}, u32[]{:S(2)}) collective-permute-start(bf16[64,3584]{1,0:T(8,128)(2,1)S(1)} %collective-permute-done.3.b), channel_id=1, source_target_pairs={{0,2},{1,7},{2,4},{3,1},{4,6},{5,3},{6,0},{7,5},{8,10},{9,15},{10,... | collective-permute-start | bytes 1376264 | tf_op jit(solution)/shard_map/ppermute | solution.py:180
  84.7 5.2 %copy-start.7 = (bf16[1,256,3584]{2,1,0:T(8,128)(2,1)S(1)}, bf16[1,256,3584]{2,1,0:T(8,128)(2,1)}, u32[]{:S(2)}) copy-start(bf16[1,256,3584]{2,1,0:T(8,128)(2,1)} %w_down.1) | copy-start | bytes 5505028
  84.8 6.4 %copy-start.2 = (bf16[256,3584]{1,0:T(8,128)(2,1)}, bf16[256,3584]{1,0:T(8,128)(2,1)S(1)}, u32[]{:S(2)}) copy-start(bf16[256,3584]{1,0:T(8,128)(2,1)S(1)} %shard_map.90.g_mine.gm) | copy-start | bytes 5505028
  84.8 5.1 %collective-permute-start.7 = (bf16[256,3584]{1,0:T(8,128)(2,1)S(1)}, bf16[256,3584]{1,0:T(8,128)(2,1)S(1)}, u32[]{:S(2)}, u32[]{:S(2)}) collective-permute-start(bf16[256,3584]{1,0:T(8,128)(2,1)S(1)} %shard_map.90.g_mine.gm), channel_id=1, source_target_pairs={{0,1},{1,0},{2,3},{3,2},{4,5},{5,4},{6,7},{7,6},{8,9},{9,8},{10,11... | collective-permute-start | bytes 5505032 | tf_op jit(solution)/shard_map/ppermute | solution.py:180
  86.5 7.9 %collective-permute-start.8 = (bf16[64,3584]{1,0:T(8,128)(2,1)}, bf16[64,3584]{1,0:T(8,128)(2,1)}, u32[]{:S(2)}, u32[]{:S(2)}) collective-permute-start(bf16[64,3584]{1,0:T(8,128)(2,1)} %get-tuple-element.46.a), channel_id=1, source_target_pairs={{0,2},{1,7},{2,4},{3,1},{4,6},{5,3},{6,0},{7,5},{8,10},{9,15},{10,... | collective-permute-start | bytes 1376264 | tf_op jit(solution)/shard_map/ppermute | solution.py:180
  89.9 1.3 copy-start.4
  95.6 5.7 %collective-permute-start.9 = (bf16[256,3584]{1,0:T(8,128)(2,1)S(1)}, bf16[256,3584]{1,0:T(8,128)(2,1)S(1)}, u32[]{:S(2)}, u32[]{:S(2)}) collective-permute-start(bf16[256,3584]{1,0:T(8,128)(2,1)S(1)} %shard_map.92), channel_id=1, source_target_pairs={{0,1},{1,0},{2,3},{3,2},{4,5},{5,4},{6,7},{7,6},{8,9},{9,8},{10,11... | collective-permute-start | bytes 5505032 | tf_op jit(solution)/shard_map/ppermute | solution.py:180
  97.8 7.8 %collective-permute-start.13 = (bf16[64,3584]{1,0:T(8,128)(2,1)}, bf16[64,3584]{1,0:T(8,128)(2,1)S(1)}, u32[]{:S(2)}, u32[]{:S(2)}) collective-permute-start(bf16[64,3584]{1,0:T(8,128)(2,1)} %collective-permute-done.8.b), channel_id=1, source_target_pairs={{0,2},{1,7},{2,4},{3,1},{4,6},{5,3},{6,0},{7,5},{8,10},{9,15},{10,... | collective-permute-start | bytes 1376264 | tf_op jit(solution)/shard_map/ppermute | solution.py:180
  98.0 38.2 %collective-permute-start.15 = (bf16[3,512,256]{2,1,0:T(8,128)(2,1)S(1)}, bf16[3,512,256]{2,1,0:T(8,128)(2,1)S(1)}, u32[]{:S(2)}, u32[]{:S(2)}) collective-permute-start(bf16[3,512,256]{2,1,0:T(8,128)(2,1)S(1)} %shard_map.91.acts), channel_id=1, source_target_pairs={{0,192},{64,128},{128,64},{192,0},{1,193},{65,129},{129,65},{193,1... | collective-permute-start | bytes 2359304 | tf_op jit(solution)/shard_map/ppermute | solution.py:201
  102.4 14.3 %collective-permute-start.10 = (bf16[64,3584]{1,0:T(8,128)(2,1)S(1)}, bf16[64,3584]{1,0:T(8,128)(2,1)S(1)}, u32[]{:S(2)}, u32[]{:S(2)}) collective-permute-start(bf16[64,3584]{1,0:T(8,128)(2,1)S(1)} %get-tuple-element.49), channel_id=1, source_target_pairs={{0,6},{1,3},{2,0},{3,5},{4,2},{5,7},{6,4},{7,1},{8,14},{9,11},{10,... | collective-permute-start | bytes 1376264 | tf_op jit(solution)/shard_map/ppermute | solution.py:180
  102.6 22.9 %collective-permute-start.11 = (bf16[64,3584]{1,0:T(8,128)(2,1)S(1)}, bf16[64,3584]{1,0:T(8,128)(2,1)S(1)}, u32[]{:S(2)}, u32[]{:S(2)}) collective-permute-start(bf16[64,3584]{1,0:T(8,128)(2,1)S(1)} %get-tuple-element.50), channel_id=1, source_target_pairs={{0,2},{1,7},{2,4},{3,1},{4,6},{5,3},{6,0},{7,5},{8,10},{9,15},{10,... | collective-permute-start | bytes 1376264 | tf_op jit(solution)/shard_map/ppermute | solution.py:180
  105.1 24.3 %collective-permute-start.12 = (bf16[64,3584]{1,0:T(8,128)(2,1)S(1)}, bf16[64,3584]{1,0:T(8,128)(2,1)S(1)}, u32[]{:S(2)}, u32[]{:S(2)}) collective-permute-start(bf16[64,3584]{1,0:T(8,128)(2,1)S(1)} %get-tuple-element.51), channel_id=1, source_target_pairs={{0,4},{1,5},{2,6},{3,7},{4,0},{5,1},{6,2},{7,3},{8,12},{9,13},{10,... | collective-permute-start | bytes 1376264 | tf_op jit(solution)/shard_map/ppermute | solution.py:180
  105.6 24.0 %copy-start.10 = (bf16[64,3584]{1,0:T(8,128)(2,1)}, bf16[64,3584]{1,0:T(8,128)(2,1)S(1)}, u32[]{:S(2)}) copy-start(bf16[64,3584]{1,0:T(8,128)(2,1)S(1)} %collective-permute-done.13.d) | copy-start | bytes 1376260
  105.6 30.5 %collective-permute-start.14 = (bf16[64,3584]{1,0:T(8,128)(2,1)}, bf16[64,3584]{1,0:T(8,128)(2,1)}, u32[]{:S(2)}, u32[]{:S(2)}) collective-permute-start(bf16[64,3584]{1,0:T(8,128)(2,1)} %get-tuple-element.46.a), channel_id=1, source_target_pairs={{0,6},{1,3},{2,0},{3,5},{4,2},{5,7},{6,4},{7,1},{8,14},{9,11},{10,... | collective-permute-start | bytes 1376264 | tf_op jit(solution)/shard_map/ppermute | solution.py:180
  116.7 22.5 %collective-permute-start.16 = (bf16[64,3584]{1,0:T(8,128)(2,1)}, bf16[64,3584]{1,0:T(8,128)(2,1)}, u32[]{:S(2)}, u32[]{:S(2)}) collective-permute-start(bf16[64,3584]{1,0:T(8,128)(2,1)} %get-tuple-element.46.a), channel_id=1, source_target_pairs={{0,1},{1,0},{2,3},{3,2},{4,5},{5,4},{6,7},{7,6},{8,9},{9,8},{10,11... | collective-permute-start | bytes 1376264 | tf_op jit(solution)/shard_map/ppermute | solution.py:180
  125.5 13.8 %collective-permute-start.17 = (bf16[64,3584]{1,0:T(8,128)(2,1)}, bf16[64,3584]{1,0:T(8,128)(2,1)}, u32[]{:S(2)}, u32[]{:S(2)}) collective-permute-start(bf16[64,3584]{1,0:T(8,128)(2,1)} %collective-permute-done.8.b), channel_id=1, source_target_pairs={{0,1},{1,0},{2,3},{3,2},{4,5},{5,4},{6,7},{7,6},{8,9},{9,8},{10,11... | collective-permute-start | bytes 1376264 | tf_op jit(solution)/shard_map/ppermute | solution.py:180
  130.4 22.2 %all-to-all-start.2 = ((bf16[8,8,3584]{2,1,0:T(8,128)(2,1)}), bf16[8,8,3584]{2,1,0:T(8,128)(2,1)}, u32[]{:S(2)}, u32[]{:S(2)}) async-start(bf16[8,8,3584]{2,1,0:T(8,128)(2,1)} %bitcast.8), calls=%async_computation.2 | async-start | bytes 917504 | tf_op jit(solution)/shard_map/all_to_all | solution.py:207
  136.2 3.1 %collective-permute-start.18 = (bf16[64,3584]{1,0:T(8,128)(2,1)}, bf16[64,3584]{1,0:T(8,128)(2,1)S(1)}, u32[]{:S(2)}, u32[]{:S(2)}) collective-permute-start(bf16[64,3584]{1,0:T(8,128)(2,1)} %collective-permute-done.14.c), channel_id=1, source_target_pairs={{0,1},{1,0},{2,3},{3,2},{4,5},{5,4},{6,7},{7,6},{8,9},{9,8},{10,11... | collective-permute-start | bytes 1376264 | tf_op jit(solution)/shard_map/ppermute | solution.py:180
  136.5 2.7 %collective-permute-start.19 = (bf16[64,3584]{1,0:T(8,128)(2,1)}, bf16[64,3584]{1,0:T(8,128)(2,1)S(1)}, u32[]{:S(2)}, u32[]{:S(2)}) collective-permute-start(bf16[64,3584]{1,0:T(8,128)(2,1)} %copy-done.10), channel_id=1, source_target_pairs={{0,1},{1,0},{2,3},{3,2},{4,5},{5,4},{6,7},{7,6},{8,9},{9,8},{10,11... | collective-permute-start | bytes 1376264 | tf_op jit(solution)/shard_map/ppermute | solution.py:180
  139.2 1.8 %copy-start.3 = (bf16[256,3584]{1,0:T(8,128)(2,1)S(1)}, bf16[256,3584]{1,0:T(8,128)(2,1)}, u32[]{:S(2)}) copy-start(bf16[256,3584]{1,0:T(8,128)(2,1)} %copy-done.2) | copy-start | bytes 5505028
  139.2 2.3 %copy-start.5 = (bf16[256,3584]{1,0:T(8,128)(2,1)S(1)}, bf16[256,3584]{1,0:T(8,128)(2,1)}, u32[]{:S(2)}) copy-start(bf16[256,3584]{1,0:T(8,128)(2,1)} %copy-done.4) | copy-start | bytes 5505028
  (6 other events, 5.4 us)
